TPU v7x, 256 devices: a whole 4x4x8 slice. The times are simulated.
256 devices in a mesh: tm: 16 (over z, x_hi), space: 16 (over x_lo, y, core).
Axes of the slice: x: 4 (x_hi: 2, x_lo: 2; x = x_hi * 2 + x_lo), y: 4, z: 8, core: 2. Of those that a mesh axis runs over, the one named last changes fastest.
Arguments:
- starts: float32 [16, 16384, 128], P('tm', 'space'), may hold values from -7.5 to 9
- region: int32 [1024, 8], P('space'), may hold values from 0 to 7
- viscosity: float32 [8], replicated, may hold values from 0.5 to 1.5
- heat_source: float32 [16384, 128], P('space'), may hold values from -2.1 to 2.1
- fine_line: float32 [128, 128], replicated, may hold values from 0 to 0.5
- coarse_line: float32 [128, 128], replicated, may hold values from 0 to 0.5
Outputs:
- ends: float32 [16, 16384, 128], P('tm', 'space')
- next_starts: float32 [16, 16384, 128], P('tm', 'space')
All inputs are finite; a program needn't handle non-finite values.
Results may differ from a plain program's by a relative error of at most 0.00012.
Values sent between devices are 32-bit elements; how exact they have to be, the bound alone decides.
No kernel may reach another device: no remote copies, remote signals or barrier semaphores. Data moves between devices by JAX's collectives and lax.ppermute only.
A program may use at most 64 MiB of HBM per device.

v0:
```python
import jax
import jax.numpy as jnp
from jax import lax
from jax.sharding import PartitionSpec as P

CELL_BLOCK = 16
REGIONS = 8
STEPS = 8


FINE_C = 0.3
FINE_R = 0.2
COARSE_C = 0.5
COARSE_R = 0.12
COARSE_Q = 3.0
SOFTEN = 0.5


def padded(cells, sides, width):
    for axis, dim in sides:
        count = lax.axis_size(axis)
        ends = count - 1
        head = lax.slice_in_dim(cells, 0, width, axis=dim)
        tail = lax.slice_in_dim(cells, cells.shape[dim] - width, cells.shape[dim], axis=dim)
        cells = jnp.concatenate(
            [
                lax.ppermute(tail, axis, [(i, (i + 1) % count) for i in range(ends)]),
                cells,
                lax.ppermute(head, axis, [((i + 1) % count, i) for i in range(ends)]),
            ],
            axis=dim,
        )
    return cells


def viscous(base, field):
    return base / (1.0 + SOFTEN * field * field)


def explicit(u_pad, m_pad, source, courant, ratio):
    middle = u_pad[1:-1]
    below = u_pad[:-2]
    above = u_pad[2:]
    face_up = 0.5 * (m_pad[1:-1] + m_pad[2:])
    face_down = 0.5 * (m_pad[1:-1] + m_pad[:-2])
    return (
        middle
        - courant * (middle - below)
        + ratio * (face_up * (above - middle) - face_down * (middle - below))
        + source
    )


def across(field, line):
    return jnp.dot(
        field, line.T, precision=lax.Precision.HIGHEST, preferred_element_type=jnp.float32
    )


def base_field(region, viscosity):
    picks = (region[:, :, None] == jnp.arange(REGIONS, dtype=jnp.int32)).astype(jnp.float32)
    blocks = jnp.sum(picks * viscosity[None, None, :], axis=2)
    rows, cols = blocks.shape
    spread = jnp.broadcast_to(blocks[:, None, :, None], (rows, CELL_BLOCK, cols, CELL_BLOCK))
    return spread.reshape(rows * CELL_BLOCK, cols * CELL_BLOCK)


def advance(state, statics, courant, ratio, weight, line):
    base_pad = statics[0]
    source_pad = weight * statics[1]
    u_pad = padded(state, (("space", 0),), 1)
    source = source_pad[1:-1]
    first = across(explicit(u_pad, viscous(base_pad, u_pad), source, courant, ratio), line)
    w_pad = padded(first, (("space", 0),), 1)
    second = viscous(base_pad, 0.5 * (u_pad + w_pad))
    return across(explicit(u_pad, second, source, courant, ratio), line)


def on_device(starts, region, viscosity, heat_source, fine_line, coarse_line):
    static_depth = 1
    base = base_field(region, viscosity)
    statics = padded(jnp.stack([base, heat_source]), (("space", 1),), static_depth)
    start = starts[0]
    state = start
    for step in range(STEPS):
        state = advance(state, statics, FINE_C, FINE_R, 1.0, fine_line)
    coarse_own = advance(start, statics, COARSE_C, COARSE_R, COARSE_Q, coarse_line)
    group = lax.axis_index("tm")
    own = jnp.where(group == 0, state, state - coarse_own)
    empty = jnp.zeros_like(start)
    every = lax.all_gather(own[None], "tm", axis=0, tiled=True)
    count = every.shape[0]

    def sweep(turn, carry):
        value, mine, before = carry
        jump = lax.dynamic_index_in_dim(every, turn, 0, keepdims=False)
        moved = advance(value, statics, COARSE_C, COARSE_R, COARSE_Q, coarse_line) + jump
        value = jnp.where(turn == 0, every[0], moved)
        mine = jnp.where(turn == group, value, mine)
        before = jnp.where(turn == group - 1, value, before)
        return (value, mine, before)

    value, mine, before = lax.fori_loop(0, count, sweep, (empty, empty, empty))
    following = jnp.where(group == 0, start, before)
    return (mine[None], following[None])


def solution(mesh):
    placed = (P("tm", "space", None), P("space", None), P(), P("space", None), P(), P())
    return jax.shard_map(
        on_device,
        mesh=mesh,
        in_specs=placed,
        out_specs=(P("tm", "space", None), P("tm", "space", None)),
        check_vma=False,
    )
```

profile of v0, /device:TPU:152, one launch (start us, length us, event | category | flops | bytes accessed | tf_op | source)
XLA Modules:
  0.0 830.7 jit_solution(15672714461184403230)
XLA Ops:
  31.3 6.4 collective-permute-start.38
  52.9 6.4 collective-permute-start.10
  65.4 6.4 collective-permute-start.12
  78.9 5.7 collective-permute-start.14
  90.5 5.8 collective-permute-start.16
  103.4 5.8 collective-permute-start.18
  115.1 5.9 collective-permute-start.20
  128.2 5.7 collective-permute-start.22
  139.8 5.8 collective-permute-start.24
  152.7 5.7 collective-permute-start.26
  164.3 5.8 collective-permute-start.28
  177.2 5.7 collective-permute-start.30
  188.8 5.8 collective-permute-start.32
  201.7 5.7 collective-permute-start.34
  214.1 5.7 collective-permute-start.36
  229.1 137.5 %all-gather.3.cloned.1.call-done = f32[16384,128]{1,0:T(8,128)} async-done(((f32[1024,128]{1,0:T(8,128)}), f32[16384,128]{1,0:T(8,128)}) %all-gather.3.cloned.1.call-update) | async-done | bytes 8388624 | tf_op jit(solution)/shard_map/all_gather | solution.py:91
  366.6 455.2 %while.20 = (s32[]{:T(128)}, f32[1024,128]{1,0:T(8,128)}, f32[1024,128]{1,0:T(8,128)}, f32[1024,128]{1,0:T(8,128)}, f32[16,1024,128]{2,1,0:T(8,128)}, /*index=5*...) while((s32[]{:T(128)}, f32[1024,128]{1,0:T(8,128)}, ...), condition=%wide.region_2.3_spmd.clone, body=%wide.region_1.2_spmd.clone.sunk | while | flops 409340416 | bytes 27946436 | solution.py:103
  376.1 4.5 collective-permute-start.2
  392.1 5.7 collective-permute-start
  403.6 5.7 collective-permute-start.2
  420.8 5.8 collective-permute-start
  432.3 5.7 collective-permute-start.2
  449.6 5.7 collective-permute-start
  461.1 5.7 collective-permute-start.2
  478.3 5.8 collective-permute-start
  489.8 5.7 collective-permute-start.2
  507.0 5.7 collective-permute-start
  518.5 5.7 collective-permute-start.2
  535.7 5.8 collective-permute-start
  547.2 5.7 collective-permute-start.2
  564.4 5.7 collective-permute-start
  575.9 5.7 collective-permute-start.2
  593.2 5.8 collective-permute-start
  604.7 5.7 collective-permute-start.2
  621.9 5.7 collective-permute-start
  633.4 5.7 collective-permute-start.2
  650.6 5.8 collective-permute-start
  662.1 5.7 collective-permute-start.2
  679.3 5.7 collective-permute-start
  690.8 5.7 collective-permute-start.2
  708.1 5.8 collective-permute-start
  719.6 5.7 collective-permute-start.2
  736.8 5.7 collective-permute-start
  748.3 5.7 collective-permute-start.2
  765.5 5.8 collective-permute-start
  777.0 5.7 collective-permute-start.2
  794.2 5.7 collective-permute-start
  805.7 5.7 collective-permute-start.2
  (636 shorter events, 411.1 us)
Async XLA Ops:
  7.2 359.5 %all-gather.3.cloned.1.call-start = ((), (), s32[]{:S(2)}) async-start(), calls=%async_computation | async-start | bytes 8912896 | tf_op jit(solution)/shard_map/all_gather | solution.py:91
  13.8 14.1 %collective-permute-start.5 = (f32[2,1,128]{2,1,0:T(1,128)S(1)}, f32[2,1,128]{2,1,0:T(1,128)S(1)}, u32[]{:S(2)}, u32[]{:S(2)}) collective-permute-start(f32[2,1,128]{2,1,0:T(1,128)S(1)} %get-tuple-element.268), channel_id=1, source_target_pairs={{0,1},{1,2},{2,3},{3,4},{4,5},{5,6},{6,7},{7,8},{8,9},{9,10},{10,1... | collective-permute-start | bytes 3080 | tf_op jit(solution)/shard_map/ppermute | solution.py:27
  15.7 12.2 %collective-permute-start.6 = (f32[2,1,128]{2,1,0:T(1,128)S(1)}, f32[2,1,128]{2,1,0:T(1,128)S(1)}, u32[]{:S(2)}, u32[]{:S(2)}) collective-permute-start(f32[2,1,128]{2,1,0:T(1,128)S(1)} %get-tuple-element.267), channel_id=1, source_target_pairs={{1,0},{2,1},{3,2},{4,3},{5,4},{6,5},{7,6},{8,7},{9,8},{10,9},{11,1... | collective-permute-start | bytes 3080 | tf_op jit(solution)/shard_map/ppermute | solution.py:29
  31.3 14.8 %collective-permute-start.38 = (f32[1,128]{1,0:T(1,128)S(1)}, f32[1,128]{1,0:T(1,128)S(1)}, u32[]{:S(2)}, u32[]{:S(2)}) collective-permute-start(f32[1,128]{1,0:T(1,128)S(1)} %get-tuple-element.270), channel_id=1, source_target_pairs={{0,1},{1,2},{2,3},{3,4},{4,5},{5,6},{6,7},{7,8},{8,9},{9,10},{10,1... | collective-permute-start | bytes 1544 | tf_op jit(solution)/shard_map/ppermute | solution.py:27
  37.6 8.5 %collective-permute-start.39 = (f32[1,128]{1,0:T(1,128)S(1)}, f32[1,128]{1,0:T(1,128)S(1)}, u32[]{:S(2)}, u32[]{:S(2)}) collective-permute-start(f32[1,128]{1,0:T(1,128)S(1)} %get-tuple-element.269), channel_id=1, source_target_pairs={{1,0},{2,1},{3,2},{4,3},{5,4},{6,5},{7,6},{8,7},{9,8},{10,9},{11,1... | collective-permute-start | bytes 1544 | tf_op jit(solution)/shard_map/ppermute | solution.py:29
  52.9 8.4 %collective-permute-start.10 = (f32[1,128]{1,0:T(1,128)S(1)}, f32[1,128]{1,0:T(1,128)S(1)}, u32[]{:S(2)}, u32[]{:S(2)}) collective-permute-start(f32[1,128]{1,0:T(1,128)S(1)} %get-tuple-element.298), channel_id=1, source_target_pairs={{0,1},{1,2},{2,3},{3,4},{4,5},{5,6},{6,7},{7,8},{8,9},{9,10},{10,1... | collective-permute-start | bytes 1544 | tf_op jit(solution)/shard_map/ppermute | solution.py:27
  65.4 8.3 collective-permute-start.12
  78.9 7.7 collective-permute-start.14
  90.5 7.7 collective-permute-start.16
  103.4 7.7 collective-permute-start.18
  115.1 7.9 collective-permute-start.20
  128.2 7.7 collective-permute-start.22
  139.8 7.7 collective-permute-start.24
  152.7 7.7 collective-permute-start.26
  164.3 7.7 collective-permute-start.28
  177.2 7.7 collective-permute-start.30
  188.8 7.7 collective-permute-start.32
  214.1 7.9 collective-permute-start.36
  392.1 7.7 collective-permute-start
  403.6 7.7 collective-permute-start.2
  420.8 7.7 collective-permute-start
  432.3 7.7 collective-permute-start.2
  449.6 7.7 collective-permute-start
  461.1 7.7 collective-permute-start.2
  478.3 7.7 collective-permute-start
  489.8 7.7 collective-permute-start.2
  507.0 7.7 collective-permute-start
  518.5 7.7 collective-permute-start.2
  535.7 7.7 collective-permute-start
  547.2 7.7 collective-permute-start.2
  564.4 7.7 collective-permute-start
  575.9 7.7 collective-permute-start.2
  593.2 7.7 collective-permute-start
  604.7 7.7 collective-permute-start.2
  621.9 7.7 collective-permute-start
  633.4 7.7 collective-permute-start.2
  650.6 7.7 collective-permute-start
  662.1 7.7 collective-permute-start.2
  679.3 7.7 collective-permute-start
  690.8 7.7 collective-permute-start.2
  708.1 7.7 collective-permute-start
  719.6 7.7 collective-permute-start.2
  736.8 7.7 collective-permute-start
  748.3 7.7 collective-permute-start.2
  765.5 7.7 collective-permute-start
  777.0 7.7 collective-permute-start.2
  794.2 7.7 collective-permute-start
  805.7 7.7 collective-permute-start.2
  (173 other events, 482.3 us)
Sparse Core Ops, SparseCore 0:
  229.2 137.4 all-gather.2
where the time goes:
time: 845 us; the launch traced here: 831 us
  starting transfers between devices  376 us (44%)
  waiting for transfers between devices  198 us (23%)
  local copies, waits for them, and re-layouts  133 us (16%)
  matrix products  80.2 us (9%)
  other arithmetic  26.4 us (3%)
  between operations  15.2 us (2%)
    ppermute x50, starting transfers between devices, padded(): lax.ppermute(tail, axis, [(i, (i + 1) % count) for i in range(ends)])  273 us
    all_gather x1, waiting for transfers between devices, on_device(): every = lax.all_gather(own[None], 'tm', axis=0, tiled=True)  138 us
    ppermute x50, starting transfers between devices, padded(): lax.ppermute(head, axis, [((i + 1) % count, i) for i in range(ends)])  103 us
    dot_general x50, matrix products, across(): jnp.dot(field, line.T, precision=lax.Precision.HIGHEST, preferred_element...  80.2 us
    concatenate x50, local copies, waits for them, and re-layouts, padded(): jnp.concatenate([lax.ppermute(tail, axis, [(i, (i + 1) % count) for i in...  67.6 us
    ppermute x50, waiting for transfers between devices, padded(): lax.ppermute(head, axis, [((i + 1) % count, i) for i in range(ends)])  60 us
    while x160, local copies, waits for them, and re-layouts  44.6 us
  transfers between devices with their start and end apart: 101, of which 49 were waited for; matrix products, arithmetic and copies ran while one was open for 1% of the time, Pallas kernels for 0%

commit v1 on v0

v1 whole, which is shorter than its diff:
```python
import functools

import jax
import jax.numpy as jnp
from jax import lax
from jax.experimental import pallas as pl
from jax.experimental.pallas import tpu as pltpu
from jax.sharding import PartitionSpec as P

NY = 128
CELL_BLOCK = 16
REGIONS = 8
STEPS = 8

FINE_C = 0.3
FINE_R = 0.2
COARSE_C = 0.5
COARSE_R = 0.12
COARSE_Q = 3.0

HALO = 48
HALO_BLOCKS = HALO // CELL_BLOCK
PACK = 2 * HALO + 8
WINDOW = 128
MARGIN = 28
BACK = WINDOW - 2 * MARGIN
VMEM_LIMIT = 48 * 1024 * 1024


def from_left(tile):
    return pltpu.roll(tile, 1, 0)


def from_right(tile):
    return pltpu.roll(tile, 7, 0)


def halves(x):
    high = x.astype(jnp.bfloat16)
    low = (x - high.astype(jnp.float32)).astype(jnp.bfloat16)
    return high, low


def line_operand(line_ref):
    high, low = halves(line_ref[...].T)
    top = jnp.concatenate([high, low], axis=1)
    return jnp.concatenate([top, top], axis=0)


def product(pairs, rhs_ref):
    left = jnp.concatenate([jnp.concatenate(halves(e), axis=1) for e in pairs], axis=0)
    both = jnp.dot(left, rhs_ref[...], preferred_element_type=jnp.float32)
    return both[:, :NY] + both[:, NY:]


def flux_pass(tiles, chunk, viscosity_of, slope_of, base_of, walls, rhs_ref, store):
    pairs = tiles // 2
    m = viscosity_of(0)
    last = m if pairs == 1 else viscosity_of(pairs - 1)
    wrapped = from_right(m[:8])
    edge = (last[8:] + wrapped) * slope_of(pairs - 1)[8:]
    before = from_left(edge)
    done, first = [], 0
    for i in range(pairs):
        if i + 1 < pairs:
            following = last if i + 1 == pairs - 1 else viscosity_of(i + 1)
            above = jnp.concatenate([m[8:], following[:8]], axis=0)
        else:
            following = None
            above = jnp.concatenate([m[8:], wrapped], axis=0)
        flux = (m + above) * slope_of(i)
        under = jnp.concatenate([before, flux[:8]], axis=0)
        e = base_of(i) + (flux - under)
        for tile, mask in walls:
            if tile // 2 == i:
                ones = jnp.ones_like(mask)
                both = [mask, ones] if tile % 2 == 0 else [ones, mask]
                e = e * jnp.concatenate(both, axis=0)
        before = flux[8:]
        m = following
        done.append(e)
        if len(done) * 2 == chunk or i + 1 == pairs:
            store(first, len(done) * 16, product(done, rhs_ref))
            done, first = [], 16 * (i + 1)


def advance(tiles, chunk, u_ref, base_ref, heat_ref, still_ref, slope_ref, w_ref, rhs_ref, courant, ratio, weight, walls, store):
    pairs = tiles // 2

    def rows(i):
        return slice(16 * i, 16 * i + 16)

    def viscosity_first(i):
        u = u_ref[rows(i), :]
        return base_ref[rows(i), :] / (2.0 + u * u)

    def viscosity_second(i):
        u = 0.5 * (u_ref[rows(i), :] + w_ref[rows(i), :])
        return base_ref[rows(i), :] / (2.0 + u * u)

    right = from_right(u_ref[0:8, :])
    difference = {}

    def step_up(i):
        if i not in difference:
            u = u_ref[rows(i), :]
            if i + 1 < pairs:
                above = u_ref[16 * i + 8 : 16 * i + 24, :]
            else:
                above = jnp.concatenate([u[8:], right], axis=0)
            difference[i] = above - u
        return difference[i]

    def slope_first(i):
        slope = ratio * step_up(i)
        slope_ref[rows(i), :] = slope
        return slope

    def still_first(i):
        up = courant * step_up(i)
        if i == 0:
            prior = from_left(courant * step_up(pairs - 1)[8:])
        else:
            prior = courant * step_up(i - 1)[8:]
        heat = heat_ref[rows(i), :]
        if weight != 1.0:
            heat = weight * heat
        still = (u_ref[rows(i), :] + heat) - jnp.concatenate([prior, up[:8]], axis=0)
        still_ref[rows(i), :] = still
        return still

    def store_first(start, count, value):
        w_ref[start : start + count, :] = value

    flux_pass(tiles, chunk, viscosity_first, slope_first, still_first, walls, rhs_ref, store_first)
    flux_pass(
        tiles,
        chunk,
        viscosity_second,
        lambda i: slope_ref[rows(i), :],
        lambda i: still_ref[rows(i), :],
        walls,
        rhs_ref,
        store,
    )


def wall(at_wall, sublane):
    row = lax.broadcasted_iota(jnp.int32, (8, NY), 0)
    return jnp.where((row == sublane) & at_wall, 0.0, 1.0)


def whole(shape):
    return pl.BlockSpec(shape, lambda: (0,) * len(shape))


ANYWHERE = pl.BlockSpec(memory_space=pl.ANY)


def pack_kernel(viscosity_ref, region_ref, start_ref, heat_ref, head_ref, tail_ref, blocks_ref, sems):
    slab = start_ref.shape[0]
    copies = [
        pltpu.make_async_copy(start_ref.at[pl.ds(0, HALO)], head_ref.at[pl.ds(0, HALO)], sems.at[0]),
        pltpu.make_async_copy(heat_ref.at[pl.ds(0, HALO)], head_ref.at[pl.ds(HALO, HALO)], sems.at[1]),
        pltpu.make_async_copy(start_ref.at[pl.ds(slab - HALO, HALO)], tail_ref.at[pl.ds(0, HALO)], sems.at[2]),
        pltpu.make_async_copy(heat_ref.at[pl.ds(slab - HALO, HALO)], tail_ref.at[pl.ds(HALO, HALO)], sems.at[3]),
    ]
    for copy in copies:
        copy.start()
    region = region_ref[...]
    count = region.shape[0]
    lane = lax.broadcasted_iota(jnp.int32, (count, NY), 1) // CELL_BLOCK
    spread = jnp.zeros((count, NY), jnp.int32)
    for col in range(NY // CELL_BLOCK):
        spread = jnp.where(lane == col, region[:, col : col + 1], spread)
    blocks = jnp.zeros((count, NY), jnp.float32)
    for value in range(REGIONS):
        blocks = jnp.where(spread == value, viscosity_ref[value], blocks)
    blocks_ref[...] = blocks
    head_ref[2 * HALO :, :] = blocks[:8]
    tail_ref[2 * HALO :, :] = blocks[count - 8 :]
    for copy in copies:
        copy.wait()


def pack(viscosity, region, start, heat):
    count = region.shape[0]
    return pl.pallas_call(
        pack_kernel,
        out_shape=(
            jax.ShapeDtypeStruct((PACK, NY), jnp.float32),
            jax.ShapeDtypeStruct((PACK, NY), jnp.float32),
            jax.ShapeDtypeStruct((count, NY), jnp.float32),
        ),
        in_specs=[pl.BlockSpec(memory_space=pltpu.SMEM), whole(region.shape), ANYWHERE, ANYWHERE],
        out_specs=(whole((PACK, NY)), whole((PACK, NY)), whole((count, NY))),
        scratch_shapes=[pltpu.SemaphoreType.DMA((4,))],
        name="pack",
    )(viscosity, region, start, heat)


def fine_kernel(
    ends,
    low_ref,
    high_ref,
    start_ref,
    heat_ref,
    blocks_ref,
    fine_ref,
    coarse_ref,
    windows_ref,
    own_ref,
    base_ref,
    source_ref,
    base_window_ref,
    source_window_ref,
    plain_u,
    plain_q,
    plain_m,
    u_ref,
    still_ref,
    slope_ref,
    w_ref,
    fine_rhs,
    coarse_rhs,
    sems,
    window_sems,
):
    space, group = lax.axis_index("space"), lax.axis_index("tm")
    slab = start_ref.shape[0]
    total = slab + 2 * HALO
    tiles = total // 8
    copies = []
    for n, (plain, part, middle) in enumerate(((plain_u, 0, start_ref), (plain_q, HALO, heat_ref))):
        copies += [
            pltpu.make_async_copy(low_ref.at[pl.ds(part, HALO)], plain.at[pl.ds(0, HALO)], sems.at[3 * n]),
            pltpu.make_async_copy(middle, plain.at[pl.ds(HALO, slab)], sems.at[3 * n + 1]),
            pltpu.make_async_copy(high_ref.at[pl.ds(part, HALO)], plain.at[pl.ds(HALO + slab, HALO)], sems.at[3 * n + 2]),
        ]
    blocks_low = pltpu.make_async_copy(low_ref.at[pl.ds(2 * HALO, 8)], still_ref.at[pl.ds(0, 8)], sems.at[6])
    blocks_high = pltpu.make_async_copy(high_ref.at[pl.ds(2 * HALO, 8)], still_ref.at[pl.ds(8, 8)], sems.at[7])
    for copy in copies + [blocks_low, blocks_high]:
        copy.start()
    fine_rhs[...] = line_operand(fine_ref)
    coarse_rhs[...] = line_operand(coarse_ref)

    def spread(block, row):
        plain_m[CELL_BLOCK * block : CELL_BLOCK * (block + 1), :] = jnp.broadcast_to(row, (CELL_BLOCK, NY))

    count = blocks_ref.shape[0]
    for b in range(count):
        spread(HALO_BLOCKS + b, blocks_ref[b : b + 1, :])
    blocks_low.wait()
    blocks_high.wait()
    for b in range(HALO_BLOCKS):
        spread(b, still_ref[8 - HALO_BLOCKS + b : 9 - HALO_BLOCKS + b, :])
        spread(HALO_BLOCKS + count + b, still_ref[8 + b : 9 + b, :])
    for copy in copies:
        copy.wait()
    corner = pl.multiple_of(group * (slab // windows_ref.shape[0]) + (HALO - (WINDOW - slab // windows_ref.shape[0]) // 2), 16)
    taken = [
        pltpu.make_async_copy(plain_m.at[pl.ds(corner, WINDOW)], base_window_ref, sems.at[0]),
        pltpu.make_async_copy(plain_q.at[pl.ds(corner, WINDOW)], source_window_ref, sems.at[1]),
    ]
    for copy in taken:
        copy.start()
    for plain, ref in ((plain_u, u_ref), (plain_q, source_ref), (plain_m, base_ref)):
        for t in range(tiles):
            ref[8 * t : 8 * t + 8, :] = plain[pl.ds(t, 8, stride=tiles), :]

    first, second = divmod(HALO - 1, tiles), divmod(HALO + slab, tiles)
    walls = [(first[1], wall(space == 0, first[0])), (second[1], wall(space == ends, second[0]))]
    chunk = 28
    fields = (u_ref, base_ref, source_ref, still_ref, slope_ref, w_ref)

    def store_own(begin, size, value):
        own_ref[begin : begin + size, :] = value

    def store_u(begin, size, value):
        u_ref[begin : begin + size, :] = value

    advance(tiles, chunk, *fields, coarse_rhs, COARSE_C, COARSE_R, COARSE_Q, walls, store_own)

    def step(_, carry):
        advance(tiles, chunk, *fields, fine_rhs, FINE_C, FINE_R, 1.0, walls, store_u)
        return carry

    lax.fori_loop(0, STEPS, step, 0)
    for t in range(tiles):
        rows = slice(8 * t, 8 * t + 8)
        value = u_ref[rows, :]
        value = jnp.where(group == 0, value, value - own_ref[rows, :])
        own_ref[rows, :] = value
        plain_u[pl.ds(t, 8, stride=tiles), :] = value
    parts = windows_ref.shape[0]
    each = slab // parts
    out = [
        pltpu.make_async_copy(
            plain_u.at[pl.ds(each * k + HALO - (WINDOW - each) // 2, WINDOW)], windows_ref.at[k], window_sems.at[k]
        )
        for k in range(parts)
    ]
    for copy in out:
        copy.start()
    for copy in taken + out:
        copy.wait()


def fine_phase(parts, ends, low, high, start, heat, blocks, fine_line, coarse_line):
    total = start.shape[0] + 2 * HALO
    field = jax.ShapeDtypeStruct((total, NY), jnp.float32)
    window = jax.ShapeDtypeStruct((WINDOW, NY), jnp.float32)
    return pl.pallas_call(
        functools.partial(fine_kernel, ends),
        out_shape=(jax.ShapeDtypeStruct((parts, WINDOW, NY), jnp.float32), field, field, field, window, window),
        in_specs=[ANYWHERE] * 4 + [whole(blocks.shape), whole((NY, NY)), whole((NY, NY))],
        out_specs=(ANYWHERE, whole(field.shape), whole(field.shape), whole(field.shape), ANYWHERE, ANYWHERE),
        scratch_shapes=[pltpu.VMEM((total, NY), jnp.float32)] * 7
        + [pltpu.VMEM((2 * NY, 2 * NY), jnp.bfloat16)] * 2
        + [pltpu.SemaphoreType.DMA((8,)), pltpu.SemaphoreType.DMA((parts,))],
        compiler_params=pltpu.CompilerParams(vmem_limit_bytes=VMEM_LIMIT),
        name="fine_phase",
    )(low, high, start, heat, blocks, fine_line, coarse_line)


def sweep_kernel(ends, jumps_ref, base_window_ref, source_window_ref, coarse_ref, back_ref, u_ref, base_ref, source_ref, still_ref, slope_ref, w_ref, plain, rhs):
    parts = jumps_ref.shape[0]
    space, part = lax.axis_index("space"), lax.axis_index("tm")
    tiles = WINDOW // 8
    rhs[...] = line_operand(coarse_ref)
    for t in range(tiles):
        rows = slice(8 * t, 8 * t + 8)
        base_ref[rows, :] = base_window_ref[pl.ds(t, 8, stride=tiles), :]
        source_ref[rows, :] = source_window_ref[pl.ds(t, 8, stride=tiles), :]
        u_ref[rows, :] = jumps_ref[0, pl.ds(t, 8, stride=tiles), :]
    back_ref[0] = jnp.zeros((BACK, NY), jnp.float32)
    back_ref[1] = jumps_ref[0, MARGIN : MARGIN + BACK, :]
    each = WINDOW // 2
    reach = (WINDOW - each) // 2
    first, second = divmod(reach - 1, tiles), divmod(reach + each, tiles)
    walls = [
        (first[1], wall((space == 0) & (part == 0), first[0])),
        (second[1], wall((space == ends) & (part == parts - 1), second[0])),
    ]
    fields = (u_ref, base_ref, source_ref, still_ref, slope_ref, w_ref)

    def turn(g, carry):
        def store(begin, size, value):
            for n in range(size // 8):
                t = begin // 8 + n
                moved = value[8 * n : 8 * n + 8] + jumps_ref[g, pl.ds(t, 8, stride=tiles), :]
                u_ref[8 * t : 8 * t + 8, :] = moved
                plain[pl.ds(t, 8, stride=tiles), :] = moved

        advance(tiles, tiles, *fields, rhs, COARSE_C, COARSE_R, COARSE_Q, walls, store)
        back_ref[g + 1] = plain[MARGIN : MARGIN + BACK, :]
        return carry

    lax.fori_loop(1, parts - 1, turn, 0)


def sweep(ends, jumps, base_window, source_window, coarse_line):
    parts = jumps.shape[0]
    window = pltpu.VMEM((WINDOW, NY), jnp.float32)
    return pl.pallas_call(
        functools.partial(sweep_kernel, ends),
        out_shape=jax.ShapeDtypeStruct((parts, BACK, NY), jnp.float32),
        in_specs=[whole(jumps.shape), whole((WINDOW, NY)), whole((WINDOW, NY)), whole((NY, NY))],
        out_specs=whole((parts, BACK, NY)),
        scratch_shapes=[window] * 7 + [pltpu.VMEM((2 * NY, 2 * NY), jnp.bfloat16)],
        compiler_params=pltpu.CompilerParams(vmem_limit_bytes=VMEM_LIMIT),
        name="sweep",
    )(jumps, base_window, source_window, coarse_line)


def last_kernel(
    ends, parts_ref, own_ref, base_ref, source_ref, start_ref, coarse_ref, ends_ref, next_ref, plain, u_ref, still_ref, slope_ref, w_ref, rhs
):
    space, group = lax.axis_index("space"), lax.axis_index("tm")
    parts = parts_ref.shape[0]
    slab = next_ref.shape[0]
    total = slab + 2 * HALO
    tiles = total // 8
    each = slab // parts
    side = (BACK - each) // 2
    rhs[...] = line_operand(coarse_ref)
    empty = jnp.zeros((HALO - 8, NY), jnp.float32)
    plain[0 : HALO - 8, :] = empty
    plain[total - HALO + 8 :, :] = empty
    gap = jnp.zeros((8 - side, NY), jnp.float32)
    plain[HALO - 8 : HALO, :] = jnp.concatenate([gap, parts_ref[0, 0:side, :]], axis=0)
    plain[HALO + slab : HALO + slab + 8, :] = jnp.concatenate([parts_ref[parts - 1, BACK - side : BACK, :], gap], axis=0)
    for k in range(parts):
        value = parts_ref[k, side : side + each, :]
        plain[HALO + each * k : HALO + each * (k + 1), :] = value
        rows = slice(each * k, each * (k + 1))
        next_ref[rows, :] = jnp.where(group == 0, start_ref[rows, :], value)
    for t in range(tiles):
        u_ref[8 * t : 8 * t + 8, :] = plain[pl.ds(t, 8, stride=tiles), :]
    first, second = divmod(HALO - 1, tiles), divmod(HALO + slab, tiles)
    walls = [(first[1], wall(space == 0, first[0])), (second[1], wall(space == ends, second[0]))]

    def store(begin, size, value):
        for n in range(size // 8):
            t = begin // 8 + n
            own = own_ref[8 * t : 8 * t + 8, :]
            moved = value[8 * n : 8 * n + 8]
            plain[pl.ds(t, 8, stride=tiles), :] = jnp.where(group == 0, own, moved + own)

    fields = (u_ref, base_ref, source_ref, still_ref, slope_ref, w_ref)
    advance(tiles, 28, *fields, rhs, COARSE_C, COARSE_R, COARSE_Q, walls, store)
    ends_ref[...] = plain[HALO : HALO + slab, :]


def last_step(ends, back, own, base, source, start, coarse_line):
    field = jax.ShapeDtypeStruct(start.shape, jnp.float32)
    total = own.shape
    return pl.pallas_call(
        functools.partial(last_kernel, ends),
        out_shape=(field, field),
        in_specs=[whole(back.shape), whole(total), whole(total), whole(total), whole(start.shape), whole((NY, NY))],
        out_specs=(whole(start.shape), whole(start.shape)),
        scratch_shapes=[pltpu.VMEM(total, jnp.float32)] * 5 + [pltpu.VMEM((2 * NY, 2 * NY), jnp.bfloat16)],
        compiler_params=pltpu.CompilerParams(vmem_limit_bytes=VMEM_LIMIT),
        name="last_step",
    )(back, own, base, source, start, coarse_line)


def on_device(starts, region, viscosity, heat_source, fine_line, coarse_line):
    start = starts[0]
    parts = lax.axis_size("tm")
    ends = lax.axis_size("space") - 1
    head, tail, blocks = pack(viscosity, region, start, heat_source)
    low = lax.ppermute(tail, "space", [(i, i + 1) for i in range(ends)])
    high = lax.ppermute(head, "space", [(i + 1, i) for i in range(ends)])
    windows, own, base, source, base_window, source_window = fine_phase(
        parts, ends, low, high, start, heat_source, blocks, fine_line, coarse_line
    )
    jumps = lax.all_to_all(windows, "tm", 0, 0)
    back = sweep(ends, jumps, base_window, source_window, coarse_line)
    mine = lax.all_to_all(back, "tm", 0, 0)
    value, following = last_step(ends, mine, own, base, source, start, coarse_line)
    return value[None], following[None]


def solution(mesh):
    placed = (P("tm", "space", None), P("space", None), P(), P("space", None), P(), P())
    return jax.shard_map(
        on_device,
        mesh=mesh,
        in_specs=placed,
        out_specs=(P("tm", "space", None), P("tm", "space", None)),
        check_vma=False,
    )
```

time: 845 us -> 97.2 us (0.12)
  the two profiles are of different devices: /device:TPU:152 before, /device:TPU:8 now
where the time goes in v1:
time: 97.2 us; the launch traced here: 96.8 us
  blocking collectives  66.9 us (69%)
  Pallas kernels  18.5 us (19%)
  starting transfers between devices  5.56 us (6%)
  local copies, waits for them, and re-layouts  3.01 us (3%)
  waiting for transfers between devices  2.08 us (2%)
    all_to_all x1, blocking collectives, on_device(): jumps = lax.all_to_all(windows, 'tm', 0, 0)  41.3 us
    all_to_all x1, blocking collectives, on_device(): mine = lax.all_to_all(back, 'tm', 0, 0)  25.6 us
    pallas_call x1, Pallas kernels, fine_phase(): pl.pallas_call(functools.partial(fine_kernel, ends), out_shape=(jax.Shape...  9.24 us
    pallas_call x1, Pallas kernels, sweep(): pl.pallas_call(functools.partial(sweep_kernel, ends), out_shape=jax.Shape...  5.18 us
    ppermute x1, starting transfers between devices, on_device(): high = lax.ppermute(head, 'space', [(i + 1, i) for i in range(ends)])  3.64 us
    unnamed x11, local copies, waits for them, and re-layouts  3.01 us
    pallas_call x1, Pallas kernels, pack(): pl.pallas_call(pack_kernel, out_shape=(jax.ShapeDtypeStruct((PACK, NY), j...  2.32 us
    ppermute x1, waiting for transfers between devices, on_device(): high = lax.ppermute(head, 'space', [(i + 1, i) for i in range(ends)])  2 us
  transfers between devices with their start and end apart: 2, of which 2 were waited for; matrix products, arithmetic and copies ran while one was open for 0% of the time, Pallas kernels for 0%

profile of v1, /device:TPU:8, one launch (start us, length us, event | category | flops | bytes accessed | tf_op | source)
XLA Modules:
  0.0 96.8 jit_solution(9232801544396241116)
XLA Ops:
  0.6 0.0 copy-start.2
  0.6 1.4 %copy.8.region_ref = s32[64,8]{1,0:T(8,128)} copy(s32[64,8]{0,1:T(8,128)} %param.7) | data formatting | bytes 4096 | tf_op args[1]
  2.0 0.0 copy-start
  2.1 0.0 copy-start.1
  2.1 2.3 %pack.1 = (f32[104,128]{1,0:T(8,128)}, f32[104,128]{1,0:T(8,128)}, f32[64,128]{1,0:T(8,128)}) custom-call(f32[8]{0:T(128)} %viscosity_ref.1, s32[64,8]{1,0:T(8,128)} %copy.8.region_ref, f32[1024,128]{1,0:T(8,128)} %bitcast.3, f32[1024,128]{1,0:T(8,128)} %heat_ref.3), custom_call_target="tpu_custom_call" | custom-call | tf_op jit(solution)/shard_map/pack/pallas_call | solution.py:188
  4.4 1.9 %collective-permute-start = (f32[104,128]{1,0:T(8,128)}, f32[104,128]{1,0:T(8,128)S(1)}, u32[]{:S(2)}, u32[]{:S(2)}) collective-permute-start(f32[104,128]{1,0:T(8,128)} %get-tuple-element.13), channel_id=1, source_target_pairs={{0,1},{1,2},{2,3},{3,4},{4,5},{5,6},{6,7},{7,8},{8,9},{9,10},{10,1... | collective-permute-start | bytes 159752 | tf_op jit(solution)/shard_map/ppermute | solution.py:434
  6.3 3.6 %collective-permute-start.1 = (f32[104,128]{1,0:T(8,128)}, f32[104,128]{1,0:T(8,128)S(1)}, u32[]{:S(2)}, u32[]{:S(2)}) collective-permute-start(f32[104,128]{1,0:T(8,128)} %get-tuple-element.14), channel_id=1, source_target_pairs={{1,0},{2,1},{3,2},{4,3},{5,4},{6,5},{7,6},{8,7},{9,8},{10,9},{11,1... | collective-permute-start | bytes 159752 | tf_op jit(solution)/shard_map/ppermute | solution.py:435
  10.0 0.1 collective-permute-done.low_ref
  10.0 2.0 %collective-permute-done.1.high_ref = f32[104,128]{1,0:T(8,128)S(1)} collective-permute-done((f32[104,128]{1,0:T(8,128)}, f32[104,128]{1,0:T(8,128)S(1)}, u32[]{:S(2)}, u32[]{:S(2)}) %collective-permute-start.1) | collective-permute-done | bytes 53280 | tf_op jit(solution)/shard_map/ppermute | solution.py:435
  12.0 0.0 copy-done.2
  12.0 0.0 copy-done
  12.0 0.0 copy-done.1
  12.1 0.0 copy-start.3
  12.1 0.8 copy-done.3
  12.9 0.0 copy-start.4
  12.9 0.8 copy-done.4
  13.7 9.2 %fine_phase.1 = (f32[16,128,128]{2,1,0:T(8,128)S(1)}, f32[1120,128]{1,0:T(8,128)S(1)}, f32[1120,128]{1,0:T(8,128)S(1)}, f32[1120,128]{1,0:T(8,128)S(1)}, f32[128,128]{1,0:T(8,128)S(1)}, /*index=5*/f32[128,128]{1,0:T(8,128)S(1)}) custom-call(f32[104,128]{1,0:T(8,128)S(1)} %collective-permute-done.low_ref, f32[104,128]{1,0:T(8,128)S(1)} %collective-permute-done.1.high_ref, ...), custom_call_target="tpu_custom_call" | custom-call | tf_op jit(solution)/shard_map/fine_phase/pallas_call | solution.py:313
  22.9 41.3 %all_to_all.10.jumps_ref = f32[16,128,128]{2,1,0:T(8,128)S(1)} all-to-all(f32[16,128,128]{2,1,0:T(8,128)S(1)} %get-tuple-element.16), channel_id=1, replica_groups=mesh['tm'=16,'space'=16] {'tm'}, dimensions={0} | all-to-all | bytes 2097152 | tf_op jit(solution)/shard_map/all_to_all | solution.py:439
  64.2 5.2 %sweep.1 = f32[16,72,128]{2,1,0:T(8,128)S(1)} custom-call(f32[16,128,128]{2,1,0:T(8,128)S(1)} %all_to_all.10.jumps_ref, f32[128,128]{1,0:T(8,128)S(1)} %get-tuple-element.17.base_window_ref, f32[128,128]{1,0:T(8,128)S(1)} %get-tuple-element.18.source_window_ref, f32[128,128]{1,0:T(8,128)S(1)} %copy-done.2), custom_call_target="tpu_custom_call" | custom-call | tf_op jit(solution)/shard_map/sweep/pallas_call | solution.py:365
  69.4 25.6 %all_to_all.11.parts_ref = f32[16,72,128]{2,1,0:T(8,128)S(1)} all-to-all(f32[16,72,128]{2,1,0:T(8,128)S(1)} %sweep.1), channel_id=1, replica_groups=mesh['tm'=16,'space'=16] {'tm'}, dimensions={0} | all-to-all | bytes 1179648 | tf_op jit(solution)/shard_map/all_to_all | solution.py:441
  95.0 1.8 %last_step.1 = (f32[1024,128]{1,0:T(8,128)}, f32[1024,128]{1,0:T(8,128)}) custom-call(f32[16,72,128]{2,1,0:T(8,128)S(1)} %all_to_all.11.parts_ref, f32[1120,128]{1,0:T(8,128)S(1)} %get-tuple-element.19.own_ref, f32[1120,128]{1,0:T(8,128)S(1)} %get-tuple-element.20.base_ref, f32[1120,128]{1,0:T(8,128)S(1)} %get-tuple-element.21.source_ref, ...), custom_call_target="tpu_custom_call" | custom-call | tf_op jit(solution)/shard_map/last_step/pallas_call | solution.py:418
Async XLA Ops:
  0.6 11.4 %copy-start.2 = (f32[128,128]{1,0:T(8,128)S(1)}, f32[128,128]{1,0:T(8,128)}, u32[]{:S(2)}) copy-start(f32[128,128]{1,0:T(8,128)} %coarse_ref.5) | copy-start | bytes 196612
  2.0 10.0 %copy-start = (f32[1,1024,128]{2,1,0:T(8,128)S(1)}, f32[1,1024,128]{2,1,0:T(8,128)}, u32[]{:S(2)}) copy-start(f32[1,1024,128]{2,1,0:T(8,128)} %param.6) | copy-start | bytes 1572868
  2.1 10.0 %copy-start.1 = (f32[1024,128]{1,0:T(8,128)S(1)}, f32[1024,128]{1,0:T(8,128)}, u32[]{:S(2)}) copy-start(f32[1024,128]{1,0:T(8,128)} %heat_ref.3) | copy-start | bytes 1572868
  4.4 5.7 %collective-permute-start = (f32[104,128]{1,0:T(8,128)}, f32[104,128]{1,0:T(8,128)S(1)}, u32[]{:S(2)}, u32[]{:S(2)}) collective-permute-start(f32[104,128]{1,0:T(8,128)} %get-tuple-element.13), channel_id=1, source_target_pairs={{0,1},{1,2},{2,3},{3,4},{4,5},{5,6},{6,7},{7,8},{8,9},{9,10},{10,1... | collective-permute-start | bytes 159752 | tf_op jit(solution)/shard_map/ppermute | solution.py:434
  6.3 5.7 %collective-permute-start.1 = (f32[104,128]{1,0:T(8,128)}, f32[104,128]{1,0:T(8,128)S(1)}, u32[]{:S(2)}, u32[]{:S(2)}) collective-permute-start(f32[104,128]{1,0:T(8,128)} %get-tuple-element.14), channel_id=1, source_target_pairs={{1,0},{2,1},{3,2},{4,3},{5,4},{6,5},{7,6},{8,7},{9,8},{10,9},{11,1... | collective-permute-start | bytes 159752 | tf_op jit(solution)/shard_map/ppermute | solution.py:435
  12.1 0.8 copy-start.3
  12.9 0.8 copy-start.4

commit v2 on v1

v2 whole, which is shorter than its diff:
```python
import functools

import jax
import jax.numpy as jnp
from jax import lax
from jax.experimental import pallas as pl
from jax.experimental.pallas import tpu as pltpu
from jax.sharding import PartitionSpec as P

NY = 128
CELL_BLOCK = 16
REGIONS = 8
STEPS = 8

FINE_C = 0.3
FINE_R = 0.2
COARSE_C = 0.5
COARSE_R = 0.12
COARSE_Q = 3.0

HALO = 48
HALO_BLOCKS = HALO // CELL_BLOCK
PACK = 2 * HALO + 8
WINDOW = 128
MARGIN = 28
BACK = WINDOW - 2 * MARGIN
GROUPS_OF_TILES = 6
VMEM_LIMIT = 16 * 1024 * 1024
SMALL_VMEM_LIMIT = 4 * 1024 * 1024


def from_left(tile):
    return pltpu.roll(tile, 1, 0)


def from_right(tile):
    return pltpu.roll(tile, 7, 0)


def halves(x):
    high = x.astype(jnp.bfloat16)
    low = (x - high.astype(jnp.float32)).astype(jnp.bfloat16)
    return high, low


def line_operand(line_ref):
    high, low = halves(line_ref[...].T)
    top = jnp.concatenate([high, low], axis=1)
    return jnp.concatenate([top, top], axis=0)


def product(pairs, rhs_ref):
    left = jnp.concatenate([jnp.concatenate(halves(e), axis=1) for e in pairs], axis=0)
    both = jnp.dot(left, rhs_ref[...], preferred_element_type=jnp.float32)
    return both[:, :NY] + both[:, NY:]


def rotated(pairs, count, turn):
    cuts = [pairs * n // count for n in range(count + 1)]
    groups = [list(range(cuts[n], cuts[n + 1])) for n in range(count)]
    return groups[turn:] + groups[:turn]


def flux_pass(groups, viscosity_of, slope_of, base_of, walls, rhs_ref, store):
    order = [i for group in groups for i in group]
    pairs = len(order)
    begin, prior = order[0], order[-1]
    m_begin = m = viscosity_of(begin)
    top = m[:8]
    if begin == 0:
        top = from_right(top)
    before = (viscosity_of(prior)[8:] + top) * slope_of(prior)[8:]
    if begin == 0:
        before = from_left(before)
    n = 0
    for group in groups:
        done = []
        for i in group:
            n += 1
            following = m_begin if n == pairs else viscosity_of(order[n])
            top = following[:8]
            if i + 1 == pairs:
                top = from_right(top)
            flux = (m + jnp.concatenate([m[8:], top], axis=0)) * slope_of(i)
            e = base_of(i) + (flux - jnp.concatenate([before, flux[:8]], axis=0))
            for tile, mask in walls:
                if tile // 2 == i:
                    ones = jnp.ones_like(mask)
                    both = [mask, ones] if tile % 2 == 0 else [ones, mask]
                    e = e * jnp.concatenate(both, axis=0)
            before = flux[8:]
            if i + 1 == pairs:
                before = from_left(before)
            m = following
            done.append(e)
        store(16 * group[0], 16 * len(group), product(done, rhs_ref))


def advance(tiles, parts, u_ref, base_ref, heat_ref, still_ref, slope_ref, w_ref, rhs_ref, courant, ratio, weight, walls, store):
    pairs = tiles // 2

    def rows(i):
        return slice(16 * i, 16 * i + 16)

    def viscosity_first(i):
        u = u_ref[rows(i), :]
        return base_ref[rows(i), :] / (2.0 + u * u)

    def viscosity_second(i):
        u = 0.5 * (u_ref[rows(i), :] + w_ref[rows(i), :])
        return base_ref[rows(i), :] / (2.0 + u * u)

    right = from_right(u_ref[0:8, :])

    def step_up(i):
        u = u_ref[rows(i), :]
        if i + 1 < pairs:
            above = u_ref[16 * i + 8 : 16 * i + 24, :]
        else:
            above = jnp.concatenate([u[8:], right], axis=0)
        return above - u

    def slope_first(i):
        return ratio * step_up(i)

    def still_first(i):
        up = step_up(i)
        slope_ref[rows(i), :] = ratio * up
        prior = from_left(step_up(pairs - 1)[8:]) if i == 0 else step_up(i - 1)[8:]
        heat = heat_ref[rows(i), :]
        if weight != 1.0:
            heat = weight * heat
        still = (u_ref[rows(i), :] + heat) - courant * jnp.concatenate([prior, up[:8]], axis=0)
        still_ref[rows(i), :] = still
        return still

    def store_first(start, count, value):
        w_ref[start : start + count, :] = value

    flux_pass(rotated(pairs, parts, 0), viscosity_first, slope_first, still_first, walls, rhs_ref, store_first)
    flux_pass(
        rotated(pairs, parts, parts // 2),
        viscosity_second,
        lambda i: slope_ref[rows(i), :],
        lambda i: still_ref[rows(i), :],
        walls,
        rhs_ref,
        store,
    )


def wall(at_wall, sublane):
    row = lax.broadcasted_iota(jnp.int32, (8, NY), 0)
    return jnp.where((row == sublane) & at_wall, 0.0, 1.0)


def whole(shape):
    return pl.BlockSpec(shape, lambda: (0,) * len(shape))


ANYWHERE = pl.BlockSpec(memory_space=pl.ANY)


def spread_blocks(viscosity_ref, region_ref):
    region = region_ref[...]
    count = region.shape[1]
    picked = jnp.zeros(region.shape, jnp.float32)
    for value in range(REGIONS):
        picked = jnp.where(region == value, viscosity_ref[value], picked)
    wide = jnp.concatenate([picked, jnp.zeros((region.shape[0], NY - count), jnp.float32)], axis=1)
    cells = [jnp.broadcast_to(wide[n : n + 1], (CELL_BLOCK, NY)) for n in range(NY // CELL_BLOCK)]
    return jnp.concatenate(cells, axis=0).T[:count]


def stay(*arrays):
    return [pltpu.with_memory_space_constraint(x, pltpu.HBM) for x in arrays]


def pack_kernel(viscosity_ref, region_ref, start_ref, heat_ref, head_ref, tail_ref, sems):
    slab = start_ref.shape[0]
    copies = []
    for n, (edge, first) in enumerate(((tail_ref, slab - HALO), (head_ref, 0))):
        for m, field in enumerate((start_ref, heat_ref)):
            target = edge.at[pl.ds(m * HALO, HALO)]
            copies.append(pltpu.make_async_copy(field.at[pl.ds(first, HALO)], target, sems.at[2 * n + m]))
    for copy in copies:
        copy.start()
    spread = spread_blocks(viscosity_ref, region_ref)
    head_ref[2 * HALO :, :] = spread[:8]
    tail_ref[2 * HALO :, :] = spread[spread.shape[0] - 8 :]
    for copy in copies:
        copy.wait()


def pack(viscosity, region, start, heat):
    edge = (PACK, NY)
    return pl.pallas_call(
        pack_kernel,
        out_shape=(jax.ShapeDtypeStruct(edge, jnp.float32), jax.ShapeDtypeStruct(edge, jnp.float32)),
        in_specs=[pl.BlockSpec(memory_space=pltpu.SMEM), whole(region.shape), ANYWHERE, ANYWHERE],
        out_specs=(whole(edge), whole(edge)),
        scratch_shapes=[pltpu.SemaphoreType.DMA((4,))],
        compiler_params=pltpu.CompilerParams(vmem_limit_bytes=SMALL_VMEM_LIMIT),
        name="pack",
    )(viscosity, region, start, heat)


def stage_kernel(viscosity_ref, region_ref, fine_ref, coarse_ref, fine_rhs, coarse_rhs, base_ref):
    spread = spread_blocks(viscosity_ref, region_ref)
    for b in range(spread.shape[0]):
        base_ref[CELL_BLOCK * b : CELL_BLOCK * (b + 1), :] = jnp.broadcast_to(spread[b : b + 1], (CELL_BLOCK, NY))
    fine_rhs[...] = line_operand(fine_ref)
    coarse_rhs[...] = line_operand(coarse_ref)


def stage(viscosity, region, fine_line, coarse_line):
    rows = region.shape[1] * CELL_BLOCK
    square = (2 * NY, 2 * NY)
    return pl.pallas_call(
        stage_kernel,
        out_shape=(
            jax.ShapeDtypeStruct(square, jnp.bfloat16),
            jax.ShapeDtypeStruct(square, jnp.bfloat16),
            jax.ShapeDtypeStruct((rows, NY), jnp.float32),
        ),
        in_specs=[pl.BlockSpec(memory_space=pltpu.SMEM), whole(region.shape), whole((NY, NY)), whole((NY, NY))],
        out_specs=(whole(square), whole(square), whole((rows, NY))),
        compiler_params=pltpu.CompilerParams(vmem_limit_bytes=SMALL_VMEM_LIMIT),
        cost_estimate=pl.CostEstimate(flops=rows * NY, bytes_accessed=8 * rows * NY, transcendentals=0),
        name="stage",
    )(viscosity, region, fine_line, coarse_line)


def fine_kernel(
    ends,
    low_ref,
    high_ref,
    start_ref,
    heat_ref,
    middle_ref,
    fine_rhs,
    coarse_rhs,
    windows_ref,
    own_ref,
    base_ref,
    source_ref,
    base_window_ref,
    source_window_ref,
    plain_u,
    plain_q,
    plain_m,
    u_ref,
    still_ref,
    slope_ref,
    w_ref,
):
    space, group = lax.axis_index("space"), lax.axis_index("tm")
    slab = start_ref.shape[0]
    total = slab + 2 * HALO
    tiles = total // 8
    for plain, part, middle in ((plain_u, 0, start_ref), (plain_q, HALO, heat_ref)):
        plain[0:HALO, :] = low_ref[part : part + HALO, :]
        plain[HALO : HALO + slab, :] = middle[...]
        plain[HALO + slab :, :] = high_ref[part : part + HALO, :]
    plain_m[HALO : HALO + slab, :] = middle_ref[...]
    for b in range(HALO_BLOCKS):
        left, right = 2 * HALO + 8 - HALO_BLOCKS + b, 2 * HALO + b
        rows = slice(CELL_BLOCK * b, CELL_BLOCK * (b + 1))
        plain_m[rows, :] = jnp.broadcast_to(low_ref[left : left + 1, :], (CELL_BLOCK, NY))
        rows = slice(HALO + slab + CELL_BLOCK * b, HALO + slab + CELL_BLOCK * (b + 1))
        plain_m[rows, :] = jnp.broadcast_to(high_ref[right : right + 1, :], (CELL_BLOCK, NY))
    parts = windows_ref.shape[0]
    each = slab // parts
    reach = (WINDOW - each) // 2
    corner = pl.multiple_of(group * each + (HALO - reach), CELL_BLOCK)
    base_window_ref[...] = plain_m[pl.ds(corner, WINDOW), :]
    source_window_ref[...] = plain_q[pl.ds(corner, WINDOW), :]
    for plain, ref in ((plain_u, u_ref), (plain_q, source_ref), (plain_m, base_ref)):
        for t in range(tiles):
            ref[8 * t : 8 * t + 8, :] = plain[pl.ds(t, 8, stride=tiles), :]

    first, second = divmod(HALO - 1, tiles), divmod(HALO + slab, tiles)
    walls = [(first[1], wall(space == 0, first[0])), (second[1], wall(space == ends, second[0]))]
    fields = (u_ref, base_ref, source_ref, still_ref, slope_ref, w_ref)

    def store_own(begin, size, value):
        own_ref[begin : begin + size, :] = value

    def store_u(begin, size, value):
        u_ref[begin : begin + size, :] = value

    advance(tiles, GROUPS_OF_TILES, *fields, coarse_rhs, COARSE_C, COARSE_R, COARSE_Q, walls, store_own)

    def step(_, carry):
        advance(tiles, GROUPS_OF_TILES, *fields, fine_rhs, FINE_C, FINE_R, 1.0, walls, store_u)
        return carry

    lax.fori_loop(0, STEPS, step, 0, unroll=4)
    for t in range(tiles):
        rows = slice(8 * t, 8 * t + 8)
        value = u_ref[rows, :]
        value = jnp.where(group == 0, value, value - own_ref[rows, :])
        own_ref[rows, :] = value
        plain_u[pl.ds(t, 8, stride=tiles), :] = value
    for k in range(parts):
        first = each * k + HALO - reach
        windows_ref[k] = plain_u[first : first + WINDOW, :]


def fine_phase(parts, ends, low, high, start, heat, base, fine_rhs, coarse_rhs):
    total = start.shape[0] + 2 * HALO
    operands = (low, high, start, heat, base, fine_rhs, coarse_rhs)
    field = jax.ShapeDtypeStruct((total, NY), jnp.float32)
    window = jax.ShapeDtypeStruct((WINDOW, NY), jnp.float32)
    return pl.pallas_call(
        functools.partial(fine_kernel, ends),
        out_shape=(jax.ShapeDtypeStruct((parts, WINDOW, NY), jnp.float32), field, field, field, window, window),
        in_specs=[whole(x.shape) for x in operands],
        out_specs=(whole((parts, WINDOW, NY)), *[whole(field.shape)] * 3, *[whole(window.shape)] * 2),
        scratch_shapes=[pltpu.VMEM((total, NY), jnp.float32)] * 7,
        compiler_params=pltpu.CompilerParams(vmem_limit_bytes=VMEM_LIMIT),
        name="fine_phase",
    )(*operands)


def sweep_kernel(ends, jumps_ref, base_window_ref, source_window_ref, rhs, back_ref, u_ref, base_ref, source_ref, still_ref, slope_ref, w_ref, plain):
    parts = jumps_ref.shape[0]
    space, part = lax.axis_index("space"), lax.axis_index("tm")
    tiles = WINDOW // 8
    for t in range(tiles):
        rows = slice(8 * t, 8 * t + 8)
        base_ref[rows, :] = base_window_ref[pl.ds(t, 8, stride=tiles), :]
        source_ref[rows, :] = source_window_ref[pl.ds(t, 8, stride=tiles), :]
        u_ref[rows, :] = jumps_ref[0, pl.ds(t, 8, stride=tiles), :]
    back_ref[0] = jnp.zeros((BACK, NY), jnp.float32)
    back_ref[1] = jumps_ref[0, MARGIN : MARGIN + BACK, :]
    each = WINDOW // 2
    reach = (WINDOW - each) // 2
    first, second = divmod(reach - 1, tiles), divmod(reach + each, tiles)
    walls = [
        (first[1], wall((space == 0) & (part == 0), first[0])),
        (second[1], wall((space == ends) & (part == parts - 1), second[0])),
    ]
    fields = (u_ref, base_ref, source_ref, still_ref, slope_ref, w_ref)

    def turn(g, carry):
        def store(begin, size, value):
            for n in range(size // 8):
                t = begin // 8 + n
                moved = value[8 * n : 8 * n + 8] + jumps_ref[g, pl.ds(t, 8, stride=tiles), :]
                u_ref[8 * t : 8 * t + 8, :] = moved
                plain[pl.ds(t, 8, stride=tiles), :] = moved

        advance(tiles, 1, *fields, rhs, COARSE_C, COARSE_R, COARSE_Q, walls, store)
        back_ref[g + 1] = plain[MARGIN : MARGIN + BACK, :]
        return carry

    lax.fori_loop(1, parts - 1, turn, 0)


def sweep(ends, jumps, base_window, source_window, coarse_rhs):
    parts = jumps.shape[0]
    window = pltpu.VMEM((WINDOW, NY), jnp.float32)
    return pl.pallas_call(
        functools.partial(sweep_kernel, ends),
        out_shape=jax.ShapeDtypeStruct((parts, BACK, NY), jnp.float32),
        in_specs=[whole(jumps.shape), whole((WINDOW, NY)), whole((WINDOW, NY)), whole(coarse_rhs.shape)],
        out_specs=whole((parts, BACK, NY)),
        scratch_shapes=[window] * 7,
        compiler_params=pltpu.CompilerParams(vmem_limit_bytes=VMEM_LIMIT),
        name="sweep",
    )(jumps, base_window, source_window, coarse_rhs)


def last_kernel(
    ends, parts_ref, own_ref, base_ref, source_ref, start_ref, rhs, ends_ref, next_ref, plain, u_ref, still_ref, slope_ref, w_ref
):
    space, group = lax.axis_index("space"), lax.axis_index("tm")
    parts = parts_ref.shape[0]
    slab = next_ref.shape[0]
    total = slab + 2 * HALO
    tiles = total // 8
    each = slab // parts
    side = (BACK - each) // 2
    empty = jnp.zeros((HALO - 8, NY), jnp.float32)
    plain[0 : HALO - 8, :] = empty
    plain[total - HALO + 8 :, :] = empty
    gap = jnp.zeros((8 - side, NY), jnp.float32)
    plain[HALO - 8 : HALO, :] = jnp.concatenate([gap, parts_ref[0, 0:side, :]], axis=0)
    plain[HALO + slab : HALO + slab + 8, :] = jnp.concatenate([parts_ref[parts - 1, BACK - side : BACK, :], gap], axis=0)
    for k in range(parts):
        value = parts_ref[k, side : side + each, :]
        plain[HALO + each * k : HALO + each * (k + 1), :] = value
        rows = slice(each * k, each * (k + 1))
        next_ref[rows, :] = jnp.where(group == 0, start_ref[rows, :], value)
    for t in range(tiles):
        u_ref[8 * t : 8 * t + 8, :] = plain[pl.ds(t, 8, stride=tiles), :]
    first, second = divmod(HALO - 1, tiles), divmod(HALO + slab, tiles)
    walls = [(first[1], wall(space == 0, first[0])), (second[1], wall(space == ends, second[0]))]

    def store(begin, size, value):
        for n in range(size // 8):
            t = begin // 8 + n
            own = own_ref[8 * t : 8 * t + 8, :]
            moved = value[8 * n : 8 * n + 8]
            plain[pl.ds(t, 8, stride=tiles), :] = jnp.where(group == 0, own, moved + own)

    fields = (u_ref, base_ref, source_ref, still_ref, slope_ref, w_ref)
    advance(tiles, GROUPS_OF_TILES, *fields, rhs, COARSE_C, COARSE_R, COARSE_Q, walls, store)
    ends_ref[...] = plain[HALO : HALO + slab, :]


def last_step(ends, back, own, base, source, start, coarse_rhs):
    field = jax.ShapeDtypeStruct(start.shape, jnp.float32)
    total = own.shape
    return pl.pallas_call(
        functools.partial(last_kernel, ends),
        out_shape=(field, field),
        in_specs=[whole(back.shape), whole(total), whole(total), whole(total), whole(start.shape), whole(coarse_rhs.shape)],
        out_specs=(whole(start.shape), whole(start.shape)),
        scratch_shapes=[pltpu.VMEM(total, jnp.float32)] * 5,
        compiler_params=pltpu.CompilerParams(vmem_limit_bytes=VMEM_LIMIT),
        name="last_step",
    )(back, own, base, source, start, coarse_rhs)


def on_device(starts, region, viscosity, heat_source, fine_line, coarse_line):
    start = starts[0]
    parts = lax.axis_size("tm")
    ends = lax.axis_size("space") - 1
    head, tail = pack(*stay(viscosity, region.T, start, heat_source))
    low = lax.ppermute(tail, "space", [(i, i + 1) for i in range(ends)])
    high = lax.ppermute(head, "space", [(i + 1, i) for i in range(ends)])
    fine_rhs, coarse_rhs, middle = stage(*stay(viscosity, region.T, fine_line, coarse_line))
    windows, own, base, source, base_window, source_window = fine_phase(
        parts, ends, low, high, start, heat_source, middle, fine_rhs, coarse_rhs
    )
    jumps = lax.all_to_all(windows, "tm", 0, 0)
    back = sweep(ends, jumps, base_window, source_window, coarse_rhs)
    mine = lax.all_to_all(back, "tm", 0, 0)
    value, following = last_step(ends, mine, own, base, source, start, coarse_rhs)
    return value[None], following[None]


def solution(mesh):
    placed = (P("tm", "space", None), P("space", None), P(), P("space", None), P(), P())
    return jax.shard_map(
        on_device,
        mesh=mesh,
        in_specs=placed,
        out_specs=(P("tm", "space", None), P("tm", "space", None)),
        check_vma=False,
    )
```

time: 97.2 us -> 91.1 us (0.937)
  local copies, waits for them, and re-layouts: 3.01 us -> 0.01 us
  Pallas kernels: 18.5 us -> 16.9 us
  waiting for transfers between devices: 2.08 us -> 0.71 us
    unnamed x11 -> x4, local copies, waits for them, and re-layouts: 3.01 us -> 0.01 us
    pallas_call x1, Pallas kernels: 9.24 us -> 7.28 us  [fine_phase(): pl.pallas_call(functools.partial(fine_kernel, ends), out_shape=(jax.Shape...]
    ppermute x1, waiting for transfers between devices: 2 us -> 0.71 us  [on_device(): high = lax.ppermute(head, 'space', [(i + 1, i) for i in range(ends)])]
    pallas_call x1 -> x2, Pallas kernels: 2.32 us -> 2.67 us  [the longest x1 1.63 us: pack(): pl.pallas_call(pack_kernel, out_shape=(jax.ShapeDtypeStruct(edge, jnp.flo...]
  transfers between devices with their start and end apart: 2 -> 2, of which waited for: 2 -> 1; matrix products, arithmetic and copies ran while one was open for 0% -> 0% of each run, Pallas kernels for 0% -> 1%
where the time goes in v2:
time: 91.1 us; the launch traced here: 90.7 us
  blocking collectives  66.9 us (73%)
  Pallas kernels  16.9 us (19%)
  starting transfers between devices  5.56 us (6%)
    all_to_all x1, blocking collectives, on_device(): jumps = lax.all_to_all(windows, 'tm', 0, 0)  41.2 us
    all_to_all x1, blocking collectives, on_device(): mine = lax.all_to_all(back, 'tm', 0, 0)  25.7 us
    pallas_call x1, Pallas kernels, fine_phase(): pl.pallas_call(functools.partial(fine_kernel, ends), out_shape=(jax.Shape...  7.28 us
    pallas_call x1, Pallas kernels, sweep(): pl.pallas_call(functools.partial(sweep_kernel, ends), out_shape=jax.Shape...  5.21 us
    ppermute x1, starting transfers between devices, on_device(): high = lax.ppermute(head, 'space', [(i + 1, i) for i in range(ends)])  3.64 us
    ppermute x1, starting transfers between devices, on_device(): low = lax.ppermute(tail, 'space', [(i, i + 1) for i in range(ends)])  1.92 us
  transfers between devices with their start and end apart: 2, of which 1 were waited for; matrix products, arithmetic and copies ran while one was open for 0% of the time, Pallas kernels for 1%

profile of v2, /device:TPU:8, one launch (start us, length us, event | category | flops | bytes accessed | tf_op | source)
XLA Modules:
  0.0 90.7 jit_solution(14171055090389303786)
XLA Ops:
  0.6 0.0 copy-start
  0.6 0.0 copy-start.1
  0.6 1.6 %pack.1 = (f32[104,128]{1,0:T(8,128)S(1)}, f32[104,128]{1,0:T(8,128)S(1)}) custom-call(f32[8]{0:T(128)} %viscosity_ref.3, s32[8,64]{1,0:T(8,128)} %bitcast.7, f32[1024,128]{1,0:T(8,128)} %bitcast.4, f32[1024,128]{1,0:T(8,128)} %heat_ref.3), custom_call_target="tpu_custom_call" | custom-call | tf_op jit(solution)/shard_map/pack/pallas_call | solution.py:197
  2.3 1.9 %collective-permute-start = (f32[104,128]{1,0:T(8,128)S(1)}, f32[104,128]{1,0:T(8,128)S(1)}, u32[]{:S(2)}, u32[]{:S(2)}) collective-permute-start(f32[104,128]{1,0:T(8,128)S(1)} %get-tuple-element.15), channel_id=1, source_target_pairs={{0,1},{1,2},{2,3},{3,4},{4,5},{5,6},{6,7},{7,8},{8,9},{9,10},{10,1... | collective-permute-start | bytes 159752 | tf_op jit(solution)/shard_map/ppermute | solution.py:432
  4.2 3.6 %collective-permute-start.1 = (f32[104,128]{1,0:T(8,128)S(1)}, f32[104,128]{1,0:T(8,128)S(1)}, u32[]{:S(2)}, u32[]{:S(2)}) collective-permute-start(f32[104,128]{1,0:T(8,128)S(1)} %get-tuple-element.16), channel_id=1, source_target_pairs={{1,0},{2,1},{3,2},{4,3},{5,4},{6,5},{7,6},{8,7},{9,8},{10,9},{11,1... | collective-permute-start | bytes 159752 | tf_op jit(solution)/shard_map/ppermute | solution.py:433
  7.9 1.0 %stage.1 = (bf16[256,256]{1,0:T(8,128)(2,1)S(1)}, bf16[256,256]{1,0:T(8,128)(2,1)S(1)}, f32[1024,128]{1,0:T(8,128)S(1)}) custom-call(f32[8]{0:T(128)} %viscosity_ref.3, s32[8,64]{1,0:T(8,128)} %bitcast.8, f32[128,128]{1,0:T(8,128)} %fine_ref.1, f32[128,128]{1,0:T(8,128)} %coarse_ref.1), custom_call_target="tpu_custom_call" | custom-call | flops 131072 | bytes 1048576 | tf_op jit(solution)/shard_map/stage/pallas_call | solution.py:219
  8.9 0.0 collective-permute-done.low_ref
  8.9 0.7 collective-permute-done.1.high_ref
  9.6 0.0 copy-done
  9.6 0.0 copy-done.1
  9.6 7.3 %fine_phase.1 = (f32[16,128,128]{2,1,0:T(8,128)S(1)}, f32[1120,128]{1,0:T(8,128)S(1)}, f32[1120,128]{1,0:T(8,128)S(1)}, f32[1120,128]{1,0:T(8,128)S(1)}, f32[128,128]{1,0:T(8,128)S(1)}, /*index=5*/f32[128,128]{1,0:T(8,128)S(1)}) custom-call(f32[104,128]{1,0:T(8,128)S(1)} %collective-permute-done.low_ref, f32[104,128]{1,0:T(8,128)S(1)} %collective-permute-done.1.high_ref, ...), custom_call_target="tpu_custom_call" | custom-call | tf_op jit(solution)/shard_map/fine_phase/pallas_call | solution.py:315
  16.9 41.2 %all_to_all.10.jumps_ref = f32[16,128,128]{2,1,0:T(8,128)S(1)} all-to-all(f32[16,128,128]{2,1,0:T(8,128)S(1)} %get-tuple-element.20), channel_id=1, replica_groups=mesh['tm'=16,'space'=16] {'tm'}, dimensions={0} | all-to-all | bytes 2097152 | tf_op jit(solution)/shard_map/all_to_all | solution.py:438
  58.1 5.2 %sweep.1 = f32[16,72,128]{2,1,0:T(8,128)S(1)} custom-call(f32[16,128,128]{2,1,0:T(8,128)S(1)} %all_to_all.10.jumps_ref, f32[128,128]{1,0:T(8,128)S(1)} %get-tuple-element.21.base_window_ref, f32[128,128]{1,0:T(8,128)S(1)} %get-tuple-element.22.source_window_ref, bf16[256,256]{1,0:T(8,128)(2,1)S(1)} %get-tuple-element.19.coarse_rhs.rhs), custom_call_target="tpu_custom_call" | custom-call | tf_op jit(solution)/shard_map/sweep/pallas_call | solution.py:364
  63.4 25.7 %all_to_all.11.parts_ref = f32[16,72,128]{2,1,0:T(8,128)S(1)} all-to-all(f32[16,72,128]{2,1,0:T(8,128)S(1)} %sweep.1), channel_id=1, replica_groups=mesh['tm'=16,'space'=16] {'tm'}, dimensions={0} | all-to-all | bytes 1179648 | tf_op jit(solution)/shard_map/all_to_all | solution.py:440
  89.0 1.7 %last_step.1 = (f32[1024,128]{1,0:T(8,128)}, f32[1024,128]{1,0:T(8,128)}) custom-call(f32[16,72,128]{2,1,0:T(8,128)S(1)} %all_to_all.11.parts_ref, f32[1120,128]{1,0:T(8,128)S(1)} %get-tuple-element.23.own_ref, f32[1120,128]{1,0:T(8,128)S(1)} %get-tuple-element.24.base_ref, f32[1120,128]{1,0:T(8,128)S(1)} %get-tuple-element.25.source_ref, ...), custom_call_target="tpu_custom_call" | custom-call | tf_op jit(solution)/shard_map/last_step/pallas_call | solution.py:416
Async XLA Ops:
  0.6 9.0 %copy-start = (f32[1,1024,128]{2,1,0:T(8,128)S(1)}, f32[1,1024,128]{2,1,0:T(8,128)}, u32[]{:S(2)}) copy-start(f32[1,1024,128]{2,1,0:T(8,128)} %param.6) | copy-start | bytes 1572868
  0.6 9.0 %copy-start.1 = (f32[1024,128]{1,0:T(8,128)S(1)}, f32[1024,128]{1,0:T(8,128)}, u32[]{:S(2)}) copy-start(f32[1024,128]{1,0:T(8,128)} %heat_ref.3) | copy-start | bytes 1572868
  2.3 6.6 %collective-permute-start = (f32[104,128]{1,0:T(8,128)S(1)}, f32[104,128]{1,0:T(8,128)S(1)}, u32[]{:S(2)}, u32[]{:S(2)}) collective-permute-start(f32[104,128]{1,0:T(8,128)S(1)} %get-tuple-element.15), channel_id=1, source_target_pairs={{0,1},{1,2},{2,3},{3,4},{4,5},{5,6},{6,7},{7,8},{8,9},{9,10},{10,1... | collective-permute-start | bytes 159752 | tf_op jit(solution)/shard_map/ppermute | solution.py:432
  4.2 5.4 %collective-permute-start.1 = (f32[104,128]{1,0:T(8,128)S(1)}, f32[104,128]{1,0:T(8,128)S(1)}, u32[]{:S(2)}, u32[]{:S(2)}) collective-permute-start(f32[104,128]{1,0:T(8,128)S(1)} %get-tuple-element.16), channel_id=1, source_target_pairs={{1,0},{2,1},{3,2},{4,3},{5,4},{6,5},{7,6},{8,7},{9,8},{10,9},{11,1... | collective-permute-start | bytes 159752 | tf_op jit(solution)/shard_map/ppermute | solution.py:433

commit v3 on v2

--- a/solution.py
+++ b/solution.py
@@ -21,10 +21,12 @@
 HALO = 48
 HALO_BLOCKS = HALO // CELL_BLOCK
 PACK = 2 * HALO + 8
-WINDOW = 128
+WINDOW = 192
 MARGIN = 28
 BACK = WINDOW - 2 * MARGIN
+BLOCKS = 2
 GROUPS_OF_TILES = 6
+SWEEP_GROUPS_OF_TILES = 2
 VMEM_LIMIT = 16 * 1024 * 1024
 SMALL_VMEM_LIMIT = 4 * 1024 * 1024
 
@@ -152,6 +154,14 @@
 def wall(at_wall, sublane):
     row = lax.broadcasted_iota(jnp.int32, (8, NY), 0)
     return jnp.where((row == sublane) & at_wall, 0.0, 1.0)
+
+
+def mirrored(part, parts):
+    return (parts // 2 - 1 - part // 2) * 2 + part % 2
+
+
+def placed(second, part, parts):
+    return jnp.where(second, mirrored(part, parts), part)
 
 
 def whole(shape):
@@ -272,15 +282,17 @@
     parts = windows_ref.shape[0]
     each = slab // parts
     reach = (WINDOW - each) // 2
-    corner = pl.multiple_of(group * each + (HALO - reach), CELL_BLOCK)
+    second = group >= parts
+    place = jnp.where(second, group - parts, group)
+    corner = pl.multiple_of(placed(second, place, parts) * each + (HALO - reach), CELL_BLOCK)
     base_window_ref[...] = plain_m[pl.ds(corner, WINDOW), :]
     source_window_ref[...] = plain_q[pl.ds(corner, WINDOW), :]
     for plain, ref in ((plain_u, u_ref), (plain_q, source_ref), (plain_m, base_ref)):
         for t in range(tiles):
             ref[8 * t : 8 * t + 8, :] = plain[pl.ds(t, 8, stride=tiles), :]
 
-    first, second = divmod(HALO - 1, tiles), divmod(HALO + slab, tiles)
-    walls = [(first[1], wall(space == 0, first[0])), (second[1], wall(space == ends, second[0]))]
+    under, over = divmod(HALO - 1, tiles), divmod(HALO + slab, tiles)
+    walls = [(under[1], wall(space == 0, under[0])), (over[1], wall(space == ends, over[0]))]
     fields = (u_ref, base_ref, source_ref, still_ref, slope_ref, w_ref)
 
     def store_own(begin, size, value):
@@ -303,8 +315,8 @@
         own_ref[rows, :] = value
         plain_u[pl.ds(t, 8, stride=tiles), :] = value
     for k in range(parts):
-        first = each * k + HALO - reach
-        windows_ref[k] = plain_u[first : first + WINDOW, :]
+        first = pl.multiple_of(placed(second, k, parts) * each + (HALO - reach), CELL_BLOCK)
+        windows_ref[k] = plain_u[pl.ds(first, WINDOW), :]
 
 
 def fine_phase(parts, ends, low, high, start, heat, base, fine_rhs, coarse_rhs):
@@ -323,23 +335,25 @@
     )(*operands)
 
 
-def sweep_kernel(ends, jumps_ref, base_window_ref, source_window_ref, rhs, back_ref, u_ref, base_ref, source_ref, still_ref, slope_ref, w_ref, plain):
+def sweep_window(ends, jumps_ref, base_window_ref, source_window_ref, rhs, back_ref, begin_ref, first, last, scratch):
+    u_ref, base_ref, source_ref, still_ref, slope_ref, w_ref, plain = scratch
     parts = jumps_ref.shape[0]
-    space, part = lax.axis_index("space"), lax.axis_index("tm")
+    space, group = lax.axis_index("space"), lax.axis_index("tm")
     tiles = WINDOW // 8
     for t in range(tiles):
         rows = slice(8 * t, 8 * t + 8)
+        u_ref[rows, :] = begin_ref[pl.ds(t, 8, stride=tiles), :]
         base_ref[rows, :] = base_window_ref[pl.ds(t, 8, stride=tiles), :]
         source_ref[rows, :] = source_window_ref[pl.ds(t, 8, stride=tiles), :]
-        u_ref[rows, :] = jumps_ref[0, pl.ds(t, 8, stride=tiles), :]
-    back_ref[0] = jnp.zeros((BACK, NY), jnp.float32)
-    back_ref[1] = jumps_ref[0, MARGIN : MARGIN + BACK, :]
-    each = WINDOW // 2
-    reach = (WINDOW - each) // 2
-    first, second = divmod(reach - 1, tiles), divmod(reach + each, tiles)
+    back_ref[first] = begin_ref[MARGIN : MARGIN + BACK, :]
+    side = HALO - CELL_BLOCK
+    each = WINDOW - 2 * side
+    second = group >= parts
+    window = placed(second, jnp.where(second, group - parts, group), parts)
+    under, over = divmod(side - 1, tiles), divmod(side + each, tiles)
     walls = [
-        (first[1], wall((space == 0) & (part == 0), first[0])),
-        (second[1], wall((space == ends) & (part == parts - 1), second[0])),
+        (under[1], wall((space == 0) & (window == 0), under[0])),
+        (over[1], wall((space == ends) & (window == parts - 1), over[0])),
     ]
     fields = (u_ref, base_ref, source_ref, still_ref, slope_ref, w_ref)
 
@@ -351,25 +365,53 @@
                 u_ref[8 * t : 8 * t + 8, :] = moved
                 plain[pl.ds(t, 8, stride=tiles), :] = moved
 
-        advance(tiles, 1, *fields, rhs, COARSE_C, COARSE_R, COARSE_Q, walls, store)
-        back_ref[g + 1] = plain[MARGIN : MARGIN + BACK, :]
+        advance(tiles, SWEEP_GROUPS_OF_TILES, *fields, rhs, COARSE_C, COARSE_R, COARSE_Q, walls, store)
+
+        @pl.when(g + 1 < parts)
+        def _():
+            back_ref[g + 1] = plain[MARGIN : MARGIN + BACK, :]
+
         return carry
 
-    lax.fori_loop(1, parts - 1, turn, 0)
-
-
-def sweep(ends, jumps, base_window, source_window, coarse_rhs):
-    parts = jumps.shape[0]
+    lax.fori_loop(first, last, turn, 0)
+
+
+def first_sweep_kernel(ends, jumps_ref, base_window_ref, source_window_ref, rhs, back_ref, over_ref, *scratch):
+    parts = jumps_ref.shape[0]
+
+    @pl.when(lax.axis_index("tm") < parts)
+    def _():
+        back_ref[0] = jnp.zeros((BACK, NY), jnp.float32)
+        windows = (jumps_ref, base_window_ref, source_window_ref, rhs)
+        sweep_window(ends, *windows, back_ref, jumps_ref.at[0], 1, parts, scratch)
+        over_ref[...] = scratch[-1][...]
+
+
+def second_sweep_kernel(ends, jumps_ref, base_window_ref, source_window_ref, rhs, first_ref, over_ref, back_ref, *scratch):
+    parts = jumps_ref.shape[0]
+    second = lax.axis_index("tm") >= parts
+
+    @pl.when(jnp.logical_not(second))
+    def _():
+        back_ref[...] = first_ref[...]
+
+    @pl.when(second)
+    def _():
+        windows = (jumps_ref, base_window_ref, source_window_ref, rhs)
+        sweep_window(ends, *windows, back_ref, over_ref, 0, parts - 1, scratch)
+
+
+def sweep(kernel, ends, outputs, *operands):
     window = pltpu.VMEM((WINDOW, NY), jnp.float32)
     return pl.pallas_call(
-        functools.partial(sweep_kernel, ends),
-        out_shape=jax.ShapeDtypeStruct((parts, BACK, NY), jnp.float32),
-        in_specs=[whole(jumps.shape), whole((WINDOW, NY)), whole((WINDOW, NY)), whole(coarse_rhs.shape)],
-        out_specs=whole((parts, BACK, NY)),
+        functools.partial(kernel, ends),
+        out_shape=tuple(jax.ShapeDtypeStruct(shape, jnp.float32) for shape in outputs),
+        in_specs=[whole(x.shape) for x in operands],
+        out_specs=tuple(whole(shape) for shape in outputs),
         scratch_shapes=[window] * 7,
         compiler_params=pltpu.CompilerParams(vmem_limit_bytes=VMEM_LIMIT),
         name="sweep",
-    )(jumps, base_window, source_window, coarse_rhs)
+    )(*operands)
 
 
 def last_kernel(
@@ -386,17 +428,20 @@
     plain[0 : HALO - 8, :] = empty
     plain[total - HALO + 8 :, :] = empty
     gap = jnp.zeros((8 - side, NY), jnp.float32)
-    plain[HALO - 8 : HALO, :] = jnp.concatenate([gap, parts_ref[0, 0:side, :]], axis=0)
-    plain[HALO + slab : HALO + slab + 8, :] = jnp.concatenate([parts_ref[parts - 1, BACK - side : BACK, :], gap], axis=0)
+    second = group >= parts
+    lowest = parts_ref[placed(second, 0, parts), 0:side, :]
+    highest = parts_ref[placed(second, parts - 1, parts), BACK - side : BACK, :]
+    plain[HALO - 8 : HALO, :] = jnp.concatenate([gap, lowest], axis=0)
+    plain[HALO + slab : HALO + slab + 8, :] = jnp.concatenate([highest, gap], axis=0)
     for k in range(parts):
-        value = parts_ref[k, side : side + each, :]
+        value = parts_ref[placed(second, k, parts), side : side + each, :]
         plain[HALO + each * k : HALO + each * (k + 1), :] = value
         rows = slice(each * k, each * (k + 1))
         next_ref[rows, :] = jnp.where(group == 0, start_ref[rows, :], value)
     for t in range(tiles):
         u_ref[8 * t : 8 * t + 8, :] = plain[pl.ds(t, 8, stride=tiles), :]
-    first, second = divmod(HALO - 1, tiles), divmod(HALO + slab, tiles)
-    walls = [(first[1], wall(space == 0, first[0])), (second[1], wall(space == ends, second[0]))]
+    under, over = divmod(HALO - 1, tiles), divmod(HALO + slab, tiles)
+    walls = [(under[1], wall(space == 0, under[0])), (over[1], wall(space == ends, over[0]))]
 
     def store(begin, size, value):
         for n in range(size // 8):
@@ -426,7 +471,9 @@
 
 def on_device(starts, region, viscosity, heat_source, fine_line, coarse_line):
     start = starts[0]
-    parts = lax.axis_size("tm")
+    groups = lax.axis_size("tm")
+    parts = groups // BLOCKS
+    members = [list(range(parts)), list(range(parts, groups))]
     ends = lax.axis_size("space") - 1
     head, tail = pack(*stay(viscosity, region.T, start, heat_source))
     low = lax.ppermute(tail, "space", [(i, i + 1) for i in range(ends)])
@@ -435,9 +482,13 @@
     windows, own, base, source, base_window, source_window = fine_phase(
         parts, ends, low, high, start, heat_source, middle, fine_rhs, coarse_rhs
     )
-    jumps = lax.all_to_all(windows, "tm", 0, 0)
-    back = sweep(ends, jumps, base_window, source_window, coarse_rhs)
-    mine = lax.all_to_all(back, "tm", 0, 0)
+    jumps = lax.all_to_all(windows, "tm", 0, 0, axis_index_groups=members)
+    back_shape = (parts, BACK, NY)
+    given = (jumps, base_window, source_window, coarse_rhs)
+    first_back, over = sweep(first_sweep_kernel, ends, (back_shape, (WINDOW, NY)), *given)
+    over = lax.ppermute(over, "tm", [(k, parts + mirrored(k, parts)) for k in range(parts)])
+    (back,) = sweep(second_sweep_kernel, ends, (back_shape,), *given, first_back, over)
+    mine = lax.all_to_all(back, "tm", 0, 0, axis_index_groups=members)
     value, following = last_step(ends, mine, own, base, source, start, coarse_rhs)
     return value[None], following[None]
 

time: 91.1 us -> 80.8 us (0.89)
  the two profiles are of different devices: /device:TPU:8 before, /device:TPU:152 now
where the time goes in v3:
time: 80.8 us; the launch traced here: 80.2 us
  blocking collectives  51.5 us (64%)
  Pallas kernels  14 us (17%)
  waiting for transfers between devices  7.13 us (9%)
  starting transfers between devices  6.84 us (8%)
    all_to_all x1, blocking collectives, on_device(): mine = lax.all_to_all(back, 'tm', 0, 0, axis_index_groups=members)  26 us
    all_to_all x1, blocking collectives, on_device(): jumps = lax.all_to_all(windows, 'tm', 0, 0, axis_index_groups=members)  25.5 us
    pallas_call x1, Pallas kernels, fine_phase(): pl.pallas_call(functools.partial(fine_kernel, ends), out_shape=(jax.Shape...  6.82 us
    ppermute x1, waiting for transfers between devices, on_device(): lax.ppermute(over, 'tm', [(k, parts + mirrored(k, parts)) for k in range(...  6.42 us
    ppermute x1, starting transfers between devices, on_device(): high = lax.ppermute(head, 'space', [(i + 1, i) for i in range(ends)])  3.64 us
    pallas_call x2, Pallas kernels, sweep(): pl.pallas_call(functools.partial(kernel, ends), out_shape=tuple((jax.Shap...  2.79 us
    ppermute x1, starting transfers between devices, on_device(): low = lax.ppermute(tail, 'space', [(i, i + 1) for i in range(ends)])  1.92 us
    pallas_call x1, Pallas kernels, last_step(): pl.pallas_call(functools.partial(last_kernel, ends), out_shape=(field, fi...  1.71 us
  transfers between devices with their start and end apart: 3, of which 2 were waited for; matrix products, arithmetic and copies ran while one was open for 0% of the time, Pallas kernels for 1%

profile of v3, /device:TPU:152, one launch (start us, length us, event | category | flops | bytes accessed | tf_op | source)
XLA Modules:
  0.0 80.2 jit_solution(14302526762136694020)
XLA Ops:
  0.6 0.0 copy-start
  0.6 0.0 copy-start.1
  0.6 1.6 %pack.1 = (f32[104,128]{1,0:T(8,128)S(1)}, f32[104,128]{1,0:T(8,128)S(1)}) custom-call(f32[8]{0:T(128)} %viscosity_ref.3, s32[8,64]{1,0:T(8,128)} %bitcast.7, f32[1024,128]{1,0:T(8,128)} %bitcast.4, f32[1024,128]{1,0:T(8,128)} %heat_ref.3), custom_call_target="tpu_custom_call" | custom-call | tf_op jit(solution)/shard_map/pack/pallas_call | solution.py:207
  2.3 1.9 %collective-permute-start = (f32[104,128]{1,0:T(8,128)S(1)}, f32[104,128]{1,0:T(8,128)S(1)}, u32[]{:S(2)}, u32[]{:S(2)}) collective-permute-start(f32[104,128]{1,0:T(8,128)S(1)} %get-tuple-element.17), channel_id=1, source_target_pairs={{0,1},{1,2},{2,3},{3,4},{4,5},{5,6},{6,7},{7,8},{8,9},{9,10},{10,1... | collective-permute-start | bytes 159752 | tf_op jit(solution)/shard_map/ppermute | solution.py:479
  4.2 3.6 %collective-permute-start.1 = (f32[104,128]{1,0:T(8,128)S(1)}, f32[104,128]{1,0:T(8,128)S(1)}, u32[]{:S(2)}, u32[]{:S(2)}) collective-permute-start(f32[104,128]{1,0:T(8,128)S(1)} %get-tuple-element.18), channel_id=1, source_target_pairs={{1,0},{2,1},{3,2},{4,3},{5,4},{6,5},{7,6},{8,7},{9,8},{10,9},{11,1... | collective-permute-start | bytes 159752 | tf_op jit(solution)/shard_map/ppermute | solution.py:480
  7.9 1.0 %stage.1 = (bf16[256,256]{1,0:T(8,128)(2,1)S(1)}, bf16[256,256]{1,0:T(8,128)(2,1)S(1)}, f32[1024,128]{1,0:T(8,128)S(1)}) custom-call(f32[8]{0:T(128)} %viscosity_ref.3, s32[8,64]{1,0:T(8,128)} %bitcast.8, f32[128,128]{1,0:T(8,128)} %fine_ref.1, f32[128,128]{1,0:T(8,128)} %coarse_ref.1), custom_call_target="tpu_custom_call" | custom-call | flops 131072 | bytes 1048576 | tf_op jit(solution)/shard_map/stage/pallas_call | solution.py:229
  8.9 0.0 collective-permute-done.low_ref
  8.9 0.7 collective-permute-done.1.high_ref
  9.6 0.0 copy-done
  9.6 0.0 copy-done.1
  9.6 6.8 %fine_phase.1 = (f32[8,192,128]{2,1,0:T(8,128)S(1)}, f32[1120,128]{1,0:T(8,128)S(1)}, f32[1120,128]{1,0:T(8,128)S(1)}, f32[1120,128]{1,0:T(8,128)S(1)}, f32[192,128]{1,0:T(8,128)S(1)}, /*index=5*/f32[192,128]{1,0:T(8,128)S(1)}) custom-call(f32[104,128]{1,0:T(8,128)S(1)} %collective-permute-done.low_ref, f32[104,128]{1,0:T(8,128)S(1)} %collective-permute-done.1.high_ref, ...), custom_call_target="tpu_custom_call" | custom-call | tf_op jit(solution)/shard_map/fine_phase/pallas_call | solution.py:327
  16.5 25.5 %all_to_all.10.jumps_ref = f32[8,192,128]{2,1,0:T(8,128)S(1)} all-to-all(f32[8,192,128]{2,1,0:T(8,128)S(1)} %get-tuple-element.22), channel_id=1, replica_groups={{0,16,32,48,64,80,96,112},{128,144,160,176,192,208,224,240},{1,17,33,49..., dimensions={0} | all-to-all | bytes 1572864 | tf_op jit(solution)/shard_map/all_to_all | solution.py:485
  42.0 1.3 %collective-permute-start.2 = (f32[192,128]{1,0:T(8,128)S(1)}, f32[192,128]{1,0:T(8,128)S(1)}, u32[]{:S(2)}, u32[]{:S(2)}) collective-permute-start(f32[192,128]{1,0:T(8,128)S(1)} %get-tuple-element.26), channel_id=1, source_target_pairs={{0,224},{16,240},{32,192},{48,208},{64,160},{80,176},{96,128},{112... | collective-permute-start | bytes 294920 | tf_op jit(solution)/shard_map/ppermute | solution.py:489
  43.3 6.4 %collective-permute-done.2.over_ref = f32[192,128]{1,0:T(8,128)S(1)} collective-permute-done((f32[192,128]{1,0:T(8,128)S(1)}, f32[192,128]{1,0:T(8,128)S(1)}, u32[]{:S(2)}, u32[]{:S(2)}) %collective-permute-start.2) | collective-permute-done | bytes 98336 | tf_op jit(solution)/shard_map/ppermute | solution.py:489
  49.7 2.8 %sweep.3 = f32[8,136,128]{2,1,0:T(8,128)S(1)} custom-call(f32[8,192,128]{2,1,0:T(8,128)S(1)} %all_to_all.10.jumps_ref, f32[192,128]{1,0:T(8,128)S(1)} %get-tuple-element.23.base_window_ref, f32[192,128]{1,0:T(8,128)S(1)} %get-tuple-element.24.source_window_ref, bf16[256,256]{1,0:T(8,128)(2,1)S(1)} %get-tuple-element.21.coarse_rhs.rhs, ...), custom_call_target="tpu_custom_call" | custom-call | tf_op jit(solution)/shard_map/sweep/pallas_call | solution.py:406
  52.5 26.0 %all_to_all.11.parts_ref = f32[8,136,128]{2,1,0:T(8,128)S(1)} all-to-all(f32[8,136,128]{2,1,0:T(8,128)S(1)} %sweep.3), channel_id=1, replica_groups={{0,16,32,48,64,80,96,112},{128,144,160,176,192,208,224,240},{1,17,33,49..., dimensions={0} | all-to-all | bytes 1114112 | tf_op jit(solution)/shard_map/all_to_all | solution.py:491
  78.5 1.7 %last_step.1 = (f32[1024,128]{1,0:T(8,128)}, f32[1024,128]{1,0:T(8,128)}) custom-call(f32[8,136,128]{2,1,0:T(8,128)S(1)} %all_to_all.11.parts_ref, f32[1120,128]{1,0:T(8,128)S(1)} %get-tuple-element.27.own_ref, f32[1120,128]{1,0:T(8,128)S(1)} %get-tuple-element.28.base_ref, f32[1120,128]{1,0:T(8,128)S(1)} %get-tuple-element.29.source_ref, ...), custom_call_target="tpu_custom_call" | custom-call | tf_op jit(solution)/shard_map/last_step/pallas_call | solution.py:461
  (1 shorter events, 0.0 us)
Async XLA Ops:
  0.6 9.0 %copy-start = (f32[1,1024,128]{2,1,0:T(8,128)S(1)}, f32[1,1024,128]{2,1,0:T(8,128)}, u32[]{:S(2)}) copy-start(f32[1,1024,128]{2,1,0:T(8,128)} %param.6) | copy-start | bytes 1572868
  0.6 9.0 %copy-start.1 = (f32[1024,128]{1,0:T(8,128)S(1)}, f32[1024,128]{1,0:T(8,128)}, u32[]{:S(2)}) copy-start(f32[1024,128]{1,0:T(8,128)} %heat_ref.3) | copy-start | bytes 1572868
  2.3 6.6 %collective-permute-start = (f32[104,128]{1,0:T(8,128)S(1)}, f32[104,128]{1,0:T(8,128)S(1)}, u32[]{:S(2)}, u32[]{:S(2)}) collective-permute-start(f32[104,128]{1,0:T(8,128)S(1)} %get-tuple-element.17), channel_id=1, source_target_pairs={{0,1},{1,2},{2,3},{3,4},{4,5},{5,6},{6,7},{7,8},{8,9},{9,10},{10,1... | collective-permute-start | bytes 159752 | tf_op jit(solution)/shard_map/ppermute | solution.py:479
  4.2 5.4 %collective-permute-start.1 = (f32[104,128]{1,0:T(8,128)S(1)}, f32[104,128]{1,0:T(8,128)S(1)}, u32[]{:S(2)}, u32[]{:S(2)}) collective-permute-start(f32[104,128]{1,0:T(8,128)S(1)} %get-tuple-element.18), channel_id=1, source_target_pairs={{1,0},{2,1},{3,2},{4,3},{5,4},{6,5},{7,6},{8,7},{9,8},{10,9},{11,1... | collective-permute-start | bytes 159752 | tf_op jit(solution)/shard_map/ppermute | solution.py:480
  42.0 7.7 %collective-permute-start.2 = (f32[192,128]{1,0:T(8,128)S(1)}, f32[192,128]{1,0:T(8,128)S(1)}, u32[]{:S(2)}, u32[]{:S(2)}) collective-permute-start(f32[192,128]{1,0:T(8,128)S(1)} %get-tuple-element.26), channel_id=1, source_target_pairs={{0,224},{16,240},{32,192},{48,208},{64,160},{80,176},{96,128},{112... | collective-permute-start | bytes 294920 | tf_op jit(solution)/shard_map/ppermute | solution.py:489

commit v4 on v3

--- a/solution.py
+++ b/solution.py
@@ -186,18 +186,21 @@
     return [pltpu.with_memory_space_constraint(x, pltpu.HBM) for x in arrays]
 
 
-def pack_kernel(viscosity_ref, region_ref, start_ref, heat_ref, head_ref, tail_ref, sems):
+def pack_kernel(viscosity_ref, region_ref, start_ref, heat_ref, outer_ref, inner_ref, sems):
     slab = start_ref.shape[0]
+    odd = lax.axis_index("space") % 2
     copies = []
-    for n, (edge, first) in enumerate(((tail_ref, slab - HALO), (head_ref, 0))):
+    for n, (edge, last) in enumerate(((outer_ref, odd), (inner_ref, 1 - odd))):
+        first = pl.multiple_of(last * (slab - HALO), CELL_BLOCK)
         for m, field in enumerate((start_ref, heat_ref)):
             target = edge.at[pl.ds(m * HALO, HALO)]
             copies.append(pltpu.make_async_copy(field.at[pl.ds(first, HALO)], target, sems.at[2 * n + m]))
     for copy in copies:
         copy.start()
     spread = spread_blocks(viscosity_ref, region_ref)
-    head_ref[2 * HALO :, :] = spread[:8]
-    tail_ref[2 * HALO :, :] = spread[spread.shape[0] - 8 :]
+    head, tail = spread[:8], spread[spread.shape[0] - 8 :]
+    outer_ref[2 * HALO :, :] = jnp.where(odd == 1, tail, head)
+    inner_ref[2 * HALO :, :] = jnp.where(odd == 1, head, tail)
     for copy in copies:
         copy.wait()
 
@@ -243,8 +246,8 @@
 
 def fine_kernel(
     ends,
-    low_ref,
-    high_ref,
+    outer_ref,
+    inner_ref,
     start_ref,
     heat_ref,
     middle_ref,
@@ -268,17 +271,26 @@
     slab = start_ref.shape[0]
     total = slab + 2 * HALO
     tiles = total // 8
+    odd = space % 2 == 1
+
+    def low(rows):
+        return jnp.where(odd, inner_ref[rows, :], outer_ref[rows, :])
+
+    def high(rows):
+        return jnp.where(odd, outer_ref[rows, :], inner_ref[rows, :])
+
     for plain, part, middle in ((plain_u, 0, start_ref), (plain_q, HALO, heat_ref)):
-        plain[0:HALO, :] = low_ref[part : part + HALO, :]
+        plain[0:HALO, :] = low(slice(part, part + HALO))
         plain[HALO : HALO + slab, :] = middle[...]
-        plain[HALO + slab :, :] = high_ref[part : part + HALO, :]
+        plain[HALO + slab :, :] = high(slice(part, part + HALO))
     plain_m[HALO : HALO + slab, :] = middle_ref[...]
+    low_blocks, high_blocks = low(slice(2 * HALO, PACK)), high(slice(2 * HALO, PACK))
     for b in range(HALO_BLOCKS):
-        left, right = 2 * HALO + 8 - HALO_BLOCKS + b, 2 * HALO + b
+        n = 8 - HALO_BLOCKS + b
         rows = slice(CELL_BLOCK * b, CELL_BLOCK * (b + 1))
-        plain_m[rows, :] = jnp.broadcast_to(low_ref[left : left + 1, :], (CELL_BLOCK, NY))
+        plain_m[rows, :] = jnp.broadcast_to(low_blocks[n : n + 1, :], (CELL_BLOCK, NY))
         rows = slice(HALO + slab + CELL_BLOCK * b, HALO + slab + CELL_BLOCK * (b + 1))
-        plain_m[rows, :] = jnp.broadcast_to(high_ref[right : right + 1, :], (CELL_BLOCK, NY))
+        plain_m[rows, :] = jnp.broadcast_to(high_blocks[b : b + 1, :], (CELL_BLOCK, NY))
     parts = windows_ref.shape[0]
     each = slab // parts
     reach = (WINDOW - each) // 2
@@ -319,9 +331,9 @@
         windows_ref[k] = plain_u[pl.ds(first, WINDOW), :]
 
 
-def fine_phase(parts, ends, low, high, start, heat, base, fine_rhs, coarse_rhs):
+def fine_phase(parts, ends, outer, inner, start, heat, base, fine_rhs, coarse_rhs):
     total = start.shape[0] + 2 * HALO
-    operands = (low, high, start, heat, base, fine_rhs, coarse_rhs)
+    operands = (outer, inner, start, heat, base, fine_rhs, coarse_rhs)
     field = jax.ShapeDtypeStruct((total, NY), jnp.float32)
     window = jax.ShapeDtypeStruct((WINDOW, NY), jnp.float32)
     return pl.pallas_call(
@@ -475,12 +487,13 @@
     parts = groups // BLOCKS
     members = [list(range(parts)), list(range(parts, groups))]
     ends = lax.axis_size("space") - 1
-    head, tail = pack(*stay(viscosity, region.T, start, heat_source))
-    low = lax.ppermute(tail, "space", [(i, i + 1) for i in range(ends)])
-    high = lax.ppermute(head, "space", [(i + 1, i) for i in range(ends)])
+    outer, inner = pack(*stay(viscosity, region.T, start, heat_source))
+    apart = [(i, i + 1) for i in range(1, ends, 2)]
+    within = [(i, i + 1) for i in range(0, ends, 2)]
+    outer, inner = (lax.ppermute(x, "space", pairs + [(j, i) for i, j in pairs]) for x, pairs in ((outer, apart), (inner, within)))
     fine_rhs, coarse_rhs, middle = stage(*stay(viscosity, region.T, fine_line, coarse_line))
     windows, own, base, source, base_window, source_window = fine_phase(
-        parts, ends, low, high, start, heat_source, middle, fine_rhs, coarse_rhs
+        parts, ends, outer, inner, start, heat_source, middle, fine_rhs, coarse_rhs
     )
     jumps = lax.all_to_all(windows, "tm", 0, 0, axis_index_groups=members)
     back_shape = (parts, BACK, NY)

time: 80.8 us -> 78.9 us (0.976)
  starting transfers between devices: 6.84 us -> 4.54 us
  waiting for transfers between devices: 7.13 us -> 8.46 us
    ppermute x2, starting transfers between devices: 5.56 us -> 3.26 us  [on_device(): lax.ppermute(x, 'space', pairs + [(j, i) for i, j in pairs])]
    all_to_all x1, blocking collectives: 26 us -> 24.2 us  [on_device(): mine = lax.all_to_all(back, 'tm', 0, 0, axis_index_groups=members)]
    all_to_all x1, blocking collectives: 25.5 us -> 26.6 us  [on_device(): jumps = lax.all_to_all(windows, 'tm', 0, 0, axis_index_groups=members)]
    ppermute x1, waiting for transfers between devices: 6.42 us -> 7.32 us  [on_device(): lax.ppermute(over, 'tm', [(k, parts + mirrored(k, parts)) for k in range(...]
where the time goes in v4:
time: 78.9 us; the launch traced here: 78.6 us
  blocking collectives  50.9 us (65%)
  Pallas kernels  14 us (18%)
  waiting for transfers between devices  8.46 us (11%)
  starting transfers between devices  4.54 us (6%)
    all_to_all x1, blocking collectives, on_device(): jumps = lax.all_to_all(windows, 'tm', 0, 0, axis_index_groups=members)  26.6 us
    all_to_all x1, blocking collectives, on_device(): mine = lax.all_to_all(back, 'tm', 0, 0, axis_index_groups=members)  24.2 us
    ppermute x1, waiting for transfers between devices, on_device(): lax.ppermute(over, 'tm', [(k, parts + mirrored(k, parts)) for k in range(...  7.32 us
    pallas_call x1, Pallas kernels, fine_phase(): pl.pallas_call(functools.partial(fine_kernel, ends), out_shape=(jax.Shape...  6.83 us
    ppermute x2, starting transfers between devices, on_device(): lax.ppermute(x, 'space', pairs + [(j, i) for i, j in pairs])  3.26 us
    pallas_call x2, Pallas kernels, sweep(): pl.pallas_call(functools.partial(kernel, ends), out_shape=tuple((jax.Shap...  2.79 us
    pallas_call x1, Pallas kernels, last_step(): pl.pallas_call(functools.partial(last_kernel, ends), out_shape=(field, fi...  1.71 us
    pallas_call x1, Pallas kernels, pack(): pl.pallas_call(pack_kernel, out_shape=(jax.ShapeDtypeStruct(edge, jnp.flo...  1.64 us
  transfers between devices with their start and end apart: 3, of which 2 were waited for; matrix products, arithmetic and copies ran while one was open for 0% of the time, Pallas kernels for 1%

profile of v4, /device:TPU:152, one launch (start us, length us, event | category | flops | bytes accessed | tf_op | source)
XLA Modules:
  0.0 78.6 jit_solution(11918402364466479042)
XLA Ops:
  0.6 0.0 copy-start
  0.6 0.0 copy-start.1
  0.6 1.6 %pack.1 = (f32[104,128]{1,0:T(8,128)S(1)}, f32[104,128]{1,0:T(8,128)S(1)}) custom-call(f32[8]{0:T(128)} %viscosity_ref.3, s32[8,64]{1,0:T(8,128)} %bitcast.7, f32[1024,128]{1,0:T(8,128)} %bitcast.4, f32[1024,128]{1,0:T(8,128)} %heat_ref.3), custom_call_target="tpu_custom_call" | custom-call | tf_op jit(solution)/shard_map/pack/pallas_call | solution.py:210
  2.3 2.1 %collective-permute-start = (f32[104,128]{1,0:T(8,128)S(1)}, f32[104,128]{1,0:T(8,128)S(1)}, u32[]{:S(2)}, u32[]{:S(2)}) collective-permute-start(f32[104,128]{1,0:T(8,128)S(1)} %get-tuple-element.17), channel_id=1, source_target_pairs={{1,2},{3,4},{5,6},{7,8},{9,10},{11,12},{13,14},{2,1},{4,3},{6,5},{... | collective-permute-start | bytes 159752 | tf_op jit(solution)/shard_map/ppermute | solution.py:493
  4.4 1.2 %collective-permute-start.1 = (f32[104,128]{1,0:T(8,128)S(1)}, f32[104,128]{1,0:T(8,128)S(1)}, u32[]{:S(2)}, u32[]{:S(2)}) collective-permute-start(f32[104,128]{1,0:T(8,128)S(1)} %get-tuple-element.18), channel_id=1, source_target_pairs={{0,1},{2,3},{4,5},{6,7},{8,9},{10,11},{12,13},{14,15},{1,0},{3,2},... | collective-permute-start | bytes 159752 | tf_op jit(solution)/shard_map/ppermute | solution.py:493
  5.6 1.0 %stage.1 = (bf16[256,256]{1,0:T(8,128)(2,1)S(1)}, bf16[256,256]{1,0:T(8,128)(2,1)S(1)}, f32[1024,128]{1,0:T(8,128)S(1)}) custom-call(f32[8]{0:T(128)} %viscosity_ref.3, s32[8,64]{1,0:T(8,128)} %bitcast.8, f32[128,128]{1,0:T(8,128)} %fine_ref.1, f32[128,128]{1,0:T(8,128)} %coarse_ref.1), custom_call_target="tpu_custom_call" | custom-call | flops 131072 | bytes 1048576 | tf_op jit(solution)/shard_map/stage/pallas_call | solution.py:232
  6.6 1.1 %collective-permute-done.outer_ref = f32[104,128]{1,0:T(8,128)S(1)} collective-permute-done((f32[104,128]{1,0:T(8,128)S(1)}, f32[104,128]{1,0:T(8,128)S(1)}, u32[]{:S(2)}, u32[]{:S(2)}) %collective-permute-start) | collective-permute-done | bytes 53280 | tf_op jit(solution)/shard_map/ppermute | solution.py:493
  7.7 0.0 collective-permute-done.1.inner_ref
  7.8 0.0 copy-done
  7.8 0.0 copy-done.1
  7.8 6.8 %fine_phase.1 = (f32[8,192,128]{2,1,0:T(8,128)S(1)}, f32[1120,128]{1,0:T(8,128)S(1)}, f32[1120,128]{1,0:T(8,128)S(1)}, f32[1120,128]{1,0:T(8,128)S(1)}, f32[192,128]{1,0:T(8,128)S(1)}, /*index=5*/f32[192,128]{1,0:T(8,128)S(1)}) custom-call(f32[104,128]{1,0:T(8,128)S(1)} %collective-permute-done.outer_ref, f32[104,128]{1,0:T(8,128)S(1)} %collective-permute-done.1.inner_ref, ...), custom_call_target="tpu_custom_call" | custom-call | tf_op jit(solution)/shard_map/fine_phase/pallas_call | solution.py:339
  14.6 26.6 %all_to_all.10.jumps_ref = f32[8,192,128]{2,1,0:T(8,128)S(1)} all-to-all(f32[8,192,128]{2,1,0:T(8,128)S(1)} %get-tuple-element.22), channel_id=1, replica_groups={{0,16,32,48,64,80,96,112},{128,144,160,176,192,208,224,240},{1,17,33,49..., dimensions={0} | all-to-all | bytes 1572864 | tf_op jit(solution)/shard_map/all_to_all | solution.py:498
  41.2 1.3 %collective-permute-start.2 = (f32[192,128]{1,0:T(8,128)S(1)}, f32[192,128]{1,0:T(8,128)S(1)}, u32[]{:S(2)}, u32[]{:S(2)}) collective-permute-start(f32[192,128]{1,0:T(8,128)S(1)} %get-tuple-element.26), channel_id=1, source_target_pairs={{0,224},{16,240},{32,192},{48,208},{64,160},{80,176},{96,128},{112... | collective-permute-start | bytes 294920 | tf_op jit(solution)/shard_map/ppermute | solution.py:502
  42.5 7.3 %collective-permute-done.2.over_ref = f32[192,128]{1,0:T(8,128)S(1)} collective-permute-done((f32[192,128]{1,0:T(8,128)S(1)}, f32[192,128]{1,0:T(8,128)S(1)}, u32[]{:S(2)}, u32[]{:S(2)}) %collective-permute-start.2) | collective-permute-done | bytes 98336 | tf_op jit(solution)/shard_map/ppermute | solution.py:502
  49.8 2.8 %sweep.3 = f32[8,136,128]{2,1,0:T(8,128)S(1)} custom-call(f32[8,192,128]{2,1,0:T(8,128)S(1)} %all_to_all.10.jumps_ref, f32[192,128]{1,0:T(8,128)S(1)} %get-tuple-element.23.base_window_ref, f32[192,128]{1,0:T(8,128)S(1)} %get-tuple-element.24.source_window_ref, bf16[256,256]{1,0:T(8,128)(2,1)S(1)} %get-tuple-element.21.coarse_rhs.rhs, ...), custom_call_target="tpu_custom_call" | custom-call | tf_op jit(solution)/shard_map/sweep/pallas_call | solution.py:418
  52.6 24.2 %all_to_all.11.parts_ref = f32[8,136,128]{2,1,0:T(8,128)S(1)} all-to-all(f32[8,136,128]{2,1,0:T(8,128)S(1)} %sweep.3), channel_id=1, replica_groups={{0,16,32,48,64,80,96,112},{128,144,160,176,192,208,224,240},{1,17,33,49..., dimensions={0} | all-to-all | bytes 1114112 | tf_op jit(solution)/shard_map/all_to_all | solution.py:504
  76.9 1.7 %last_step.1 = (f32[1024,128]{1,0:T(8,128)}, f32[1024,128]{1,0:T(8,128)}) custom-call(f32[8,136,128]{2,1,0:T(8,128)S(1)} %all_to_all.11.parts_ref, f32[1120,128]{1,0:T(8,128)S(1)} %get-tuple-element.27.own_ref, f32[1120,128]{1,0:T(8,128)S(1)} %get-tuple-element.28.base_ref, f32[1120,128]{1,0:T(8,128)S(1)} %get-tuple-element.29.source_ref, ...), custom_call_target="tpu_custom_call" | custom-call | tf_op jit(solution)/shard_map/last_step/pallas_call | solution.py:473
  (1 shorter events, 0.0 us)
Async XLA Ops:
  0.6 7.1 %copy-start = (f32[1,1024,128]{2,1,0:T(8,128)S(1)}, f32[1,1024,128]{2,1,0:T(8,128)}, u32[]{:S(2)}) copy-start(f32[1,1024,128]{2,1,0:T(8,128)} %param.6) | copy-start | bytes 1572868
  0.6 7.1 %copy-start.1 = (f32[1024,128]{1,0:T(8,128)S(1)}, f32[1024,128]{1,0:T(8,128)}, u32[]{:S(2)}) copy-start(f32[1024,128]{1,0:T(8,128)} %heat_ref.3) | copy-start | bytes 1572868
  2.3 5.5 %collective-permute-start = (f32[104,128]{1,0:T(8,128)S(1)}, f32[104,128]{1,0:T(8,128)S(1)}, u32[]{:S(2)}, u32[]{:S(2)}) collective-permute-start(f32[104,128]{1,0:T(8,128)S(1)} %get-tuple-element.17), channel_id=1, source_target_pairs={{1,2},{3,4},{5,6},{7,8},{9,10},{11,12},{13,14},{2,1},{4,3},{6,5},{... | collective-permute-start | bytes 159752 | tf_op jit(solution)/shard_map/ppermute | solution.py:493
  4.4 3.4 %collective-permute-start.1 = (f32[104,128]{1,0:T(8,128)S(1)}, f32[104,128]{1,0:T(8,128)S(1)}, u32[]{:S(2)}, u32[]{:S(2)}) collective-permute-start(f32[104,128]{1,0:T(8,128)S(1)} %get-tuple-element.18), channel_id=1, source_target_pairs={{0,1},{2,3},{4,5},{6,7},{8,9},{10,11},{12,13},{14,15},{1,0},{3,2},... | collective-permute-start | bytes 159752 | tf_op jit(solution)/shard_map/ppermute | solution.py:493
  41.2 8.6 %collective-permute-start.2 = (f32[192,128]{1,0:T(8,128)S(1)}, f32[192,128]{1,0:T(8,128)S(1)}, u32[]{:S(2)}, u32[]{:S(2)}) collective-permute-start(f32[192,128]{1,0:T(8,128)S(1)} %get-tuple-element.26), channel_id=1, source_target_pairs={{0,224},{16,240},{32,192},{48,208},{64,160},{80,176},{96,128},{112... | collective-permute-start | bytes 294920 | tf_op jit(solution)/shard_map/ppermute | solution.py:502

commit v5 on v4

--- a/solution.py
+++ b/solution.py
@@ -24,6 +24,7 @@
 WINDOW = 192
 MARGIN = 28
 BACK = WINDOW - 2 * MARGIN
+OVER = WINDOW - 16
 BLOCKS = 2
 GROUPS_OF_TILES = 6
 SWEEP_GROUPS_OF_TILES = 2
@@ -98,14 +99,31 @@
         store(16 * group[0], 16 * len(group), product(done, rhs_ref))
 
 
+def recent(compute, count):
+    kept = {}
+
+    def call(i):
+        if i in kept:
+            kept[i] = kept.pop(i)
+        else:
+            kept[i] = compute(i)
+            if len(kept) > count:
+                del kept[next(iter(kept))]
+        return kept[i]
+
+    return call
+
+
 def advance(tiles, parts, u_ref, base_ref, heat_ref, still_ref, slope_ref, w_ref, rhs_ref, courant, ratio, weight, walls, store):
     pairs = tiles // 2
 
     def rows(i):
         return slice(16 * i, 16 * i + 16)
 
+    u_at = recent(lambda i: u_ref[rows(i), :], 3)
+
     def viscosity_first(i):
-        u = u_ref[rows(i), :]
+        u = u_at(i)
         return base_ref[rows(i), :] / (2.0 + u * u)
 
     def viscosity_second(i):
@@ -114,13 +132,12 @@
 
     right = from_right(u_ref[0:8, :])
 
-    def step_up(i):
-        u = u_ref[rows(i), :]
-        if i + 1 < pairs:
-            above = u_ref[16 * i + 8 : 16 * i + 24, :]
-        else:
-            above = jnp.concatenate([u[8:], right], axis=0)
-        return above - u
+    def step(i):
+        u = u_at(i)
+        top = u_at(i + 1)[:8] if i + 1 < pairs else right
+        return jnp.concatenate([u[8:], top], axis=0) - u
+
+    step_up = recent(step, 2)
 
     def slope_first(i):
         return ratio * step_up(i)
@@ -132,7 +149,7 @@
         heat = heat_ref[rows(i), :]
         if weight != 1.0:
             heat = weight * heat
-        still = (u_ref[rows(i), :] + heat) - courant * jnp.concatenate([prior, up[:8]], axis=0)
+        still = (u_at(i) + heat) - courant * jnp.concatenate([prior, up[:8]], axis=0)
         still_ref[rows(i), :] = still
         return still
 
@@ -319,7 +336,7 @@
         advance(tiles, GROUPS_OF_TILES, *fields, fine_rhs, FINE_C, FINE_R, 1.0, walls, store_u)
         return carry
 
-    lax.fori_loop(0, STEPS, step, 0, unroll=4)
+    lax.fori_loop(0, STEPS, step, 0, unroll=STEPS)
     for t in range(tiles):
         rows = slice(8 * t, 8 * t + 8)
         value = u_ref[rows, :]
@@ -396,7 +413,7 @@
         back_ref[0] = jnp.zeros((BACK, NY), jnp.float32)
         windows = (jumps_ref, base_window_ref, source_window_ref, rhs)
         sweep_window(ends, *windows, back_ref, jumps_ref.at[0], 1, parts, scratch)
-        over_ref[...] = scratch[-1][...]
+        over_ref[...] = scratch[-1][8 : 8 + OVER, :]
 
 
 def second_sweep_kernel(ends, jumps_ref, base_window_ref, source_window_ref, rhs, first_ref, over_ref, back_ref, *scratch):
@@ -410,7 +427,12 @@
     @pl.when(second)
     def _():
         windows = (jumps_ref, base_window_ref, source_window_ref, rhs)
-        sweep_window(ends, *windows, back_ref, over_ref, 0, parts - 1, scratch)
+        begin_ref = scratch[-1]
+        unused = jnp.zeros((8, NY), jnp.float32)
+        begin_ref[0:8, :] = unused
+        begin_ref[8 : 8 + OVER, :] = over_ref[...]
+        begin_ref[8 + OVER :, :] = unused
+        sweep_window(ends, *windows, back_ref, begin_ref, 0, parts - 1, scratch)
 
 
 def sweep(kernel, ends, outputs, *operands):
@@ -498,7 +520,7 @@
     jumps = lax.all_to_all(windows, "tm", 0, 0, axis_index_groups=members)
     back_shape = (parts, BACK, NY)
     given = (jumps, base_window, source_window, coarse_rhs)
-    first_back, over = sweep(first_sweep_kernel, ends, (back_shape, (WINDOW, NY)), *given)
+    first_back, over = sweep(first_sweep_kernel, ends, (back_shape, (OVER, NY)), *given)
     over = lax.ppermute(over, "tm", [(k, parts + mirrored(k, parts)) for k in range(parts)])
     (back,) = sweep(second_sweep_kernel, ends, (back_shape,), *given, first_back, over)
     mine = lax.all_to_all(back, "tm", 0, 0, axis_index_groups=members)

time: 78.9 us -> 78.1 us (0.990)
  no operation moved by 1% of the time
where the time goes in v5:
time: 78.1 us; the launch traced here: 77.8 us
  blocking collectives  50.7 us (65%)
  Pallas kernels  13.6 us (17%)
  waiting for transfers between devices  8.28 us (11%)
  starting transfers between devices  4.54 us (6%)
    all_to_all x1, blocking collectives, on_device(): jumps = lax.all_to_all(windows, 'tm', 0, 0, axis_index_groups=members)  26.6 us
    all_to_all x1, blocking collectives, on_device(): mine = lax.all_to_all(back, 'tm', 0, 0, axis_index_groups=members)  24.1 us
    ppermute x1, waiting for transfers between devices, on_device(): lax.ppermute(over, 'tm', [(k, parts + mirrored(k, parts)) for k in range(...  7.13 us
    pallas_call x1, Pallas kernels, fine_phase(): pl.pallas_call(functools.partial(fine_kernel, ends), out_shape=(jax.Shape...  6.45 us
    ppermute x2, starting transfers between devices, on_device(): lax.ppermute(x, 'space', pairs + [(j, i) for i, j in pairs])  3.26 us
    pallas_call x2, Pallas kernels, sweep(): pl.pallas_call(functools.partial(kernel, ends), out_shape=tuple((jax.Shap...  2.75 us
    pallas_call x1, Pallas kernels, last_step(): pl.pallas_call(functools.partial(last_kernel, ends), out_shape=(field, fi...  1.71 us
    pallas_call x1, Pallas kernels, pack(): pl.pallas_call(pack_kernel, out_shape=(jax.ShapeDtypeStruct(edge, jnp.flo...  1.64 us
  transfers between devices with their start and end apart: 3, of which 2 were waited for; matrix products, arithmetic and copies ran while one was open for 0% of the time, Pallas kernels for 1%

profile of v5, /device:TPU:152, one launch (start us, length us, event | category | flops | bytes accessed | tf_op | source)
XLA Modules:
  0.0 77.8 jit_solution(1663923645281220105)
XLA Ops:
  0.6 0.0 copy-start
  0.6 0.0 copy-start.1
  0.6 1.6 %pack.1 = (f32[104,128]{1,0:T(8,128)S(1)}, f32[104,128]{1,0:T(8,128)S(1)}) custom-call(f32[8]{0:T(128)} %viscosity_ref.3, s32[8,64]{1,0:T(8,128)} %bitcast.7, f32[1024,128]{1,0:T(8,128)} %bitcast.4, f32[1024,128]{1,0:T(8,128)} %heat_ref.3), custom_call_target="tpu_custom_call" | custom-call | tf_op jit(solution)/shard_map/pack/pallas_call | solution.py:227
  2.3 2.1 %collective-permute-start = (f32[104,128]{1,0:T(8,128)S(1)}, f32[104,128]{1,0:T(8,128)S(1)}, u32[]{:S(2)}, u32[]{:S(2)}) collective-permute-start(f32[104,128]{1,0:T(8,128)S(1)} %get-tuple-element.17), channel_id=1, source_target_pairs={{1,2},{3,4},{5,6},{7,8},{9,10},{11,12},{13,14},{2,1},{4,3},{6,5},{... | collective-permute-start | bytes 159752 | tf_op jit(solution)/shard_map/ppermute | solution.py:515
  4.4 1.2 %collective-permute-start.1 = (f32[104,128]{1,0:T(8,128)S(1)}, f32[104,128]{1,0:T(8,128)S(1)}, u32[]{:S(2)}, u32[]{:S(2)}) collective-permute-start(f32[104,128]{1,0:T(8,128)S(1)} %get-tuple-element.18), channel_id=1, source_target_pairs={{0,1},{2,3},{4,5},{6,7},{8,9},{10,11},{12,13},{14,15},{1,0},{3,2},... | collective-permute-start | bytes 159752 | tf_op jit(solution)/shard_map/ppermute | solution.py:515
  5.6 1.0 %stage.1 = (bf16[256,256]{1,0:T(8,128)(2,1)S(1)}, bf16[256,256]{1,0:T(8,128)(2,1)S(1)}, f32[1024,128]{1,0:T(8,128)S(1)}) custom-call(f32[8]{0:T(128)} %viscosity_ref.3, s32[8,64]{1,0:T(8,128)} %bitcast.8, f32[128,128]{1,0:T(8,128)} %fine_ref.1, f32[128,128]{1,0:T(8,128)} %coarse_ref.1), custom_call_target="tpu_custom_call" | custom-call | flops 131072 | bytes 1048576 | tf_op jit(solution)/shard_map/stage/pallas_call | solution.py:249
  6.6 1.1 %collective-permute-done.outer_ref = f32[104,128]{1,0:T(8,128)S(1)} collective-permute-done((f32[104,128]{1,0:T(8,128)S(1)}, f32[104,128]{1,0:T(8,128)S(1)}, u32[]{:S(2)}, u32[]{:S(2)}) %collective-permute-start) | collective-permute-done | bytes 53280 | tf_op jit(solution)/shard_map/ppermute | solution.py:515
  7.7 0.0 collective-permute-done.1.inner_ref
  7.8 0.0 copy-done
  7.8 0.0 copy-done.1
  7.8 6.4 %fine_phase.1 = (f32[8,192,128]{2,1,0:T(8,128)S(1)}, f32[1120,128]{1,0:T(8,128)S(1)}, f32[1120,128]{1,0:T(8,128)S(1)}, f32[1120,128]{1,0:T(8,128)S(1)}, f32[192,128]{1,0:T(8,128)S(1)}, /*index=5*/f32[192,128]{1,0:T(8,128)S(1)}) custom-call(f32[104,128]{1,0:T(8,128)S(1)} %collective-permute-done.outer_ref, f32[104,128]{1,0:T(8,128)S(1)} %collective-permute-done.1.inner_ref, ...), custom_call_target="tpu_custom_call" | custom-call | tf_op jit(solution)/shard_map/fine_phase/pallas_call | solution.py:356
  14.2 26.6 %all_to_all.10.jumps_ref = f32[8,192,128]{2,1,0:T(8,128)S(1)} all-to-all(f32[8,192,128]{2,1,0:T(8,128)S(1)} %get-tuple-element.22), channel_id=1, replica_groups={{0,16,32,48,64,80,96,112},{128,144,160,176,192,208,224,240},{1,17,33,49..., dimensions={0} | all-to-all | bytes 1572864 | tf_op jit(solution)/shard_map/all_to_all | solution.py:520
  40.8 1.3 %collective-permute-start.2 = (f32[176,128]{1,0:T(8,128)S(1)}, f32[176,128]{1,0:T(8,128)S(1)}, u32[]{:S(2)}, u32[]{:S(2)}) collective-permute-start(f32[176,128]{1,0:T(8,128)S(1)} %get-tuple-element.26), channel_id=1, source_target_pairs={{0,224},{16,240},{32,192},{48,208},{64,160},{80,176},{96,128},{112... | collective-permute-start | bytes 270344 | tf_op jit(solution)/shard_map/ppermute | solution.py:524
  42.1 7.1 %collective-permute-done.2.over_ref = f32[176,128]{1,0:T(8,128)S(1)} collective-permute-done((f32[176,128]{1,0:T(8,128)S(1)}, f32[176,128]{1,0:T(8,128)S(1)}, u32[]{:S(2)}, u32[]{:S(2)}) %collective-permute-start.2) | collective-permute-done | bytes 90144 | tf_op jit(solution)/shard_map/ppermute | solution.py:524
  49.3 2.8 %sweep.3 = f32[8,136,128]{2,1,0:T(8,128)S(1)} custom-call(f32[8,192,128]{2,1,0:T(8,128)S(1)} %all_to_all.10.jumps_ref, f32[192,128]{1,0:T(8,128)S(1)} %get-tuple-element.23.base_window_ref, f32[192,128]{1,0:T(8,128)S(1)} %get-tuple-element.24.source_window_ref, bf16[256,256]{1,0:T(8,128)(2,1)S(1)} %get-tuple-element.21.coarse_rhs.rhs, ...), custom_call_target="tpu_custom_call" | custom-call | tf_op jit(solution)/shard_map/sweep/pallas_call | solution.py:440
  52.0 24.1 %all_to_all.11.parts_ref = f32[8,136,128]{2,1,0:T(8,128)S(1)} all-to-all(f32[8,136,128]{2,1,0:T(8,128)S(1)} %sweep.3), channel_id=1, replica_groups={{0,16,32,48,64,80,96,112},{128,144,160,176,192,208,224,240},{1,17,33,49..., dimensions={0} | all-to-all | bytes 1114112 | tf_op jit(solution)/shard_map/all_to_all | solution.py:526
  76.1 1.7 %last_step.1 = (f32[1024,128]{1,0:T(8,128)}, f32[1024,128]{1,0:T(8,128)}) custom-call(f32[8,136,128]{2,1,0:T(8,128)S(1)} %all_to_all.11.parts_ref, f32[1120,128]{1,0:T(8,128)S(1)} %get-tuple-element.27.own_ref, f32[1120,128]{1,0:T(8,128)S(1)} %get-tuple-element.28.base_ref, f32[1120,128]{1,0:T(8,128)S(1)} %get-tuple-element.29.source_ref, ...), custom_call_target="tpu_custom_call" | custom-call | tf_op jit(solution)/shard_map/last_step/pallas_call | solution.py:495
  (1 shorter events, 0.0 us)
Async XLA Ops:
  0.6 7.1 %copy-start = (f32[1,1024,128]{2,1,0:T(8,128)S(1)}, f32[1,1024,128]{2,1,0:T(8,128)}, u32[]{:S(2)}) copy-start(f32[1,1024,128]{2,1,0:T(8,128)} %param.6) | copy-start | bytes 1572868
  0.6 7.1 %copy-start.1 = (f32[1024,128]{1,0:T(8,128)S(1)}, f32[1024,128]{1,0:T(8,128)}, u32[]{:S(2)}) copy-start(f32[1024,128]{1,0:T(8,128)} %heat_ref.3) | copy-start | bytes 1572868
  2.3 5.5 %collective-permute-start = (f32[104,128]{1,0:T(8,128)S(1)}, f32[104,128]{1,0:T(8,128)S(1)}, u32[]{:S(2)}, u32[]{:S(2)}) collective-permute-start(f32[104,128]{1,0:T(8,128)S(1)} %get-tuple-element.17), channel_id=1, source_target_pairs={{1,2},{3,4},{5,6},{7,8},{9,10},{11,12},{13,14},{2,1},{4,3},{6,5},{... | collective-permute-start | bytes 159752 | tf_op jit(solution)/shard_map/ppermute | solution.py:515
  4.4 3.4 %collective-permute-start.1 = (f32[104,128]{1,0:T(8,128)S(1)}, f32[104,128]{1,0:T(8,128)S(1)}, u32[]{:S(2)}, u32[]{:S(2)}) collective-permute-start(f32[104,128]{1,0:T(8,128)S(1)} %get-tuple-element.18), channel_id=1, source_target_pairs={{0,1},{2,3},{4,5},{6,7},{8,9},{10,11},{12,13},{14,15},{1,0},{3,2},... | collective-permute-start | bytes 159752 | tf_op jit(solution)/shard_map/ppermute | solution.py:515
  40.8 8.4 %collective-permute-start.2 = (f32[176,128]{1,0:T(8,128)S(1)}, f32[176,128]{1,0:T(8,128)S(1)}, u32[]{:S(2)}, u32[]{:S(2)}) collective-permute-start(f32[176,128]{1,0:T(8,128)S(1)} %get-tuple-element.26), channel_id=1, source_target_pairs={{0,224},{16,240},{32,192},{48,208},{64,160},{80,176},{96,128},{112... | collective-permute-start | bytes 270344 | tf_op jit(solution)/shard_map/ppermute | solution.py:524

commit v6 on v5

--- a/solution.py
+++ b/solution.py
@@ -386,7 +386,7 @@
     ]
     fields = (u_ref, base_ref, source_ref, still_ref, slope_ref, w_ref)
 
-    def turn(g, carry):
+    def turn(g):
         def store(begin, size, value):
             for n in range(size // 8):
                 t = begin // 8 + n
@@ -395,14 +395,11 @@
                 plain[pl.ds(t, 8, stride=tiles), :] = moved
 
         advance(tiles, SWEEP_GROUPS_OF_TILES, *fields, rhs, COARSE_C, COARSE_R, COARSE_Q, walls, store)
-
-        @pl.when(g + 1 < parts)
-        def _():
+        if g + 1 < parts:
             back_ref[g + 1] = plain[MARGIN : MARGIN + BACK, :]
 
-        return carry
-
-    lax.fori_loop(first, last, turn, 0)
+    for g in range(first, last):
+        turn(g)
 
 
 def first_sweep_kernel(ends, jumps_ref, base_window_ref, source_window_ref, rhs, back_ref, over_ref, *scratch):

time: 78.1 us -> 77.9 us (level)
  no operation moved by 1% of the time
where the time goes in v6:
time: 77.9 us; the launch traced here: 77.6 us
  blocking collectives  50.7 us (65%)
  Pallas kernels  13.3 us (17%)
  waiting for transfers between devices  8.28 us (11%)
  starting transfers between devices  4.54 us (6%)
    all_to_all x1, blocking collectives, on_device(): jumps = lax.all_to_all(windows, 'tm', 0, 0, axis_index_groups=members)  26.6 us
    all_to_all x1, blocking collectives, on_device(): mine = lax.all_to_all(back, 'tm', 0, 0, axis_index_groups=members)  24.1 us
    ppermute x1, waiting for transfers between devices, on_device(): lax.ppermute(over, 'tm', [(k, parts + mirrored(k, parts)) for k in range(...  7.13 us
    pallas_call x1, Pallas kernels, fine_phase(): pl.pallas_call(functools.partial(fine_kernel, ends), out_shape=(jax.Shape...  6.45 us
    ppermute x2, starting transfers between devices, on_device(): lax.ppermute(x, 'space', pairs + [(j, i) for i, j in pairs])  3.26 us
    pallas_call x2, Pallas kernels, sweep(): pl.pallas_call(functools.partial(kernel, ends), out_shape=tuple((jax.Shap...  2.51 us
    pallas_call x1, Pallas kernels, last_step(): pl.pallas_call(functools.partial(last_kernel, ends), out_shape=(field, fi...  1.71 us
    pallas_call x1, Pallas kernels, pack(): pl.pallas_call(pack_kernel, out_shape=(jax.ShapeDtypeStruct(edge, jnp.flo...  1.64 us
  transfers between devices with their start and end apart: 3, of which 2 were waited for; matrix products, arithmetic and copies ran while one was open for 0% of the time, Pallas kernels for 1%

profile of v6, /device:TPU:152, one launch (start us, length us, event | category | flops | bytes accessed | tf_op | source)
XLA Modules:
  0.0 77.6 jit_solution(15042746358469696820)
XLA Ops:
  0.6 0.0 copy-start
  0.6 0.0 copy-start.1
  0.6 1.6 %pack.1 = (f32[104,128]{1,0:T(8,128)S(1)}, f32[104,128]{1,0:T(8,128)S(1)}) custom-call(f32[8]{0:T(128)} %viscosity_ref.3, s32[8,64]{1,0:T(8,128)} %bitcast.7, f32[1024,128]{1,0:T(8,128)} %bitcast.4, f32[1024,128]{1,0:T(8,128)} %heat_ref.3), custom_call_target="tpu_custom_call" | custom-call | tf_op jit(solution)/shard_map/pack/pallas_call | solution.py:227
  2.3 2.1 %collective-permute-start = (f32[104,128]{1,0:T(8,128)S(1)}, f32[104,128]{1,0:T(8,128)S(1)}, u32[]{:S(2)}, u32[]{:S(2)}) collective-permute-start(f32[104,128]{1,0:T(8,128)S(1)} %get-tuple-element.17), channel_id=1, source_target_pairs={{1,2},{3,4},{5,6},{7,8},{9,10},{11,12},{13,14},{2,1},{4,3},{6,5},{... | collective-permute-start | bytes 159752 | tf_op jit(solution)/shard_map/ppermute | solution.py:512
  4.4 1.2 %collective-permute-start.1 = (f32[104,128]{1,0:T(8,128)S(1)}, f32[104,128]{1,0:T(8,128)S(1)}, u32[]{:S(2)}, u32[]{:S(2)}) collective-permute-start(f32[104,128]{1,0:T(8,128)S(1)} %get-tuple-element.18), channel_id=1, source_target_pairs={{0,1},{2,3},{4,5},{6,7},{8,9},{10,11},{12,13},{14,15},{1,0},{3,2},... | collective-permute-start | bytes 159752 | tf_op jit(solution)/shard_map/ppermute | solution.py:512
  5.6 1.0 %stage.1 = (bf16[256,256]{1,0:T(8,128)(2,1)S(1)}, bf16[256,256]{1,0:T(8,128)(2,1)S(1)}, f32[1024,128]{1,0:T(8,128)S(1)}) custom-call(f32[8]{0:T(128)} %viscosity_ref.3, s32[8,64]{1,0:T(8,128)} %bitcast.8, f32[128,128]{1,0:T(8,128)} %fine_ref.1, f32[128,128]{1,0:T(8,128)} %coarse_ref.1), custom_call_target="tpu_custom_call" | custom-call | flops 131072 | bytes 1048576 | tf_op jit(solution)/shard_map/stage/pallas_call | solution.py:249
  6.6 1.1 %collective-permute-done.outer_ref = f32[104,128]{1,0:T(8,128)S(1)} collective-permute-done((f32[104,128]{1,0:T(8,128)S(1)}, f32[104,128]{1,0:T(8,128)S(1)}, u32[]{:S(2)}, u32[]{:S(2)}) %collective-permute-start) | collective-permute-done | bytes 53280 | tf_op jit(solution)/shard_map/ppermute | solution.py:512
  7.7 0.0 collective-permute-done.1.inner_ref
  7.8 0.0 copy-done
  7.8 0.0 copy-done.1
  7.8 6.4 %fine_phase.1 = (f32[8,192,128]{2,1,0:T(8,128)S(1)}, f32[1120,128]{1,0:T(8,128)S(1)}, f32[1120,128]{1,0:T(8,128)S(1)}, f32[1120,128]{1,0:T(8,128)S(1)}, f32[192,128]{1,0:T(8,128)S(1)}, /*index=5*/f32[192,128]{1,0:T(8,128)S(1)}) custom-call(f32[104,128]{1,0:T(8,128)S(1)} %collective-permute-done.outer_ref, f32[104,128]{1,0:T(8,128)S(1)} %collective-permute-done.1.inner_ref, ...), custom_call_target="tpu_custom_call" | custom-call | tf_op jit(solution)/shard_map/fine_phase/pallas_call | solution.py:356
  14.2 26.6 %all_to_all.10.jumps_ref = f32[8,192,128]{2,1,0:T(8,128)S(1)} all-to-all(f32[8,192,128]{2,1,0:T(8,128)S(1)} %get-tuple-element.22), channel_id=1, replica_groups={{0,16,32,48,64,80,96,112},{128,144,160,176,192,208,224,240},{1,17,33,49..., dimensions={0} | all-to-all | bytes 1572864 | tf_op jit(solution)/shard_map/all_to_all | solution.py:517
  40.8 1.3 %collective-permute-start.2 = (f32[176,128]{1,0:T(8,128)S(1)}, f32[176,128]{1,0:T(8,128)S(1)}, u32[]{:S(2)}, u32[]{:S(2)}) collective-permute-start(f32[176,128]{1,0:T(8,128)S(1)} %get-tuple-element.26), channel_id=1, source_target_pairs={{0,224},{16,240},{32,192},{48,208},{64,160},{80,176},{96,128},{112... | collective-permute-start | bytes 270344 | tf_op jit(solution)/shard_map/ppermute | solution.py:521
  42.1 7.1 %collective-permute-done.2.over_ref = f32[176,128]{1,0:T(8,128)S(1)} collective-permute-done((f32[176,128]{1,0:T(8,128)S(1)}, f32[176,128]{1,0:T(8,128)S(1)}, u32[]{:S(2)}, u32[]{:S(2)}) %collective-permute-start.2) | collective-permute-done | bytes 90144 | tf_op jit(solution)/shard_map/ppermute | solution.py:521
  49.3 2.5 %sweep.3 = f32[8,136,128]{2,1,0:T(8,128)S(1)} custom-call(f32[8,192,128]{2,1,0:T(8,128)S(1)} %all_to_all.10.jumps_ref, f32[192,128]{1,0:T(8,128)S(1)} %get-tuple-element.23.base_window_ref, f32[192,128]{1,0:T(8,128)S(1)} %get-tuple-element.24.source_window_ref, bf16[256,256]{1,0:T(8,128)(2,1)S(1)} %get-tuple-element.21.coarse_rhs.rhs, ...), custom_call_target="tpu_custom_call" | custom-call | tf_op jit(solution)/shard_map/sweep/pallas_call | solution.py:437
  51.8 24.1 %all_to_all.11.parts_ref = f32[8,136,128]{2,1,0:T(8,128)S(1)} all-to-all(f32[8,136,128]{2,1,0:T(8,128)S(1)} %sweep.3), channel_id=1, replica_groups={{0,16,32,48,64,80,96,112},{128,144,160,176,192,208,224,240},{1,17,33,49..., dimensions={0} | all-to-all | bytes 1114112 | tf_op jit(solution)/shard_map/all_to_all | solution.py:523
  75.9 1.7 %last_step.1 = (f32[1024,128]{1,0:T(8,128)}, f32[1024,128]{1,0:T(8,128)}) custom-call(f32[8,136,128]{2,1,0:T(8,128)S(1)} %all_to_all.11.parts_ref, f32[1120,128]{1,0:T(8,128)S(1)} %get-tuple-element.27.own_ref, f32[1120,128]{1,0:T(8,128)S(1)} %get-tuple-element.28.base_ref, f32[1120,128]{1,0:T(8,128)S(1)} %get-tuple-element.29.source_ref, ...), custom_call_target="tpu_custom_call" | custom-call | tf_op jit(solution)/shard_map/last_step/pallas_call | solution.py:492
  (1 shorter events, 0.0 us)
Async XLA Ops:
  0.6 7.1 %copy-start = (f32[1,1024,128]{2,1,0:T(8,128)S(1)}, f32[1,1024,128]{2,1,0:T(8,128)}, u32[]{:S(2)}) copy-start(f32[1,1024,128]{2,1,0:T(8,128)} %param.6) | copy-start | bytes 1572868
  0.6 7.1 %copy-start.1 = (f32[1024,128]{1,0:T(8,128)S(1)}, f32[1024,128]{1,0:T(8,128)}, u32[]{:S(2)}) copy-start(f32[1024,128]{1,0:T(8,128)} %heat_ref.3) | copy-start | bytes 1572868
  2.3 5.5 %collective-permute-start = (f32[104,128]{1,0:T(8,128)S(1)}, f32[104,128]{1,0:T(8,128)S(1)}, u32[]{:S(2)}, u32[]{:S(2)}) collective-permute-start(f32[104,128]{1,0:T(8,128)S(1)} %get-tuple-element.17), channel_id=1, source_target_pairs={{1,2},{3,4},{5,6},{7,8},{9,10},{11,12},{13,14},{2,1},{4,3},{6,5},{... | collective-permute-start | bytes 159752 | tf_op jit(solution)/shard_map/ppermute | solution.py:512
  4.4 3.4 %collective-permute-start.1 = (f32[104,128]{1,0:T(8,128)S(1)}, f32[104,128]{1,0:T(8,128)S(1)}, u32[]{:S(2)}, u32[]{:S(2)}) collective-permute-start(f32[104,128]{1,0:T(8,128)S(1)} %get-tuple-element.18), channel_id=1, source_target_pairs={{0,1},{2,3},{4,5},{6,7},{8,9},{10,11},{12,13},{14,15},{1,0},{3,2},... | collective-permute-start | bytes 159752 | tf_op jit(solution)/shard_map/ppermute | solution.py:512
  40.8 8.4 %collective-permute-start.2 = (f32[176,128]{1,0:T(8,128)S(1)}, f32[176,128]{1,0:T(8,128)S(1)}, u32[]{:S(2)}, u32[]{:S(2)}) collective-permute-start(f32[176,128]{1,0:T(8,128)S(1)} %get-tuple-element.26), channel_id=1, source_target_pairs={{0,224},{16,240},{32,192},{48,208},{64,160},{80,176},{96,128},{112... | collective-permute-start | bytes 270344 | tf_op jit(solution)/shard_map/ppermute | solution.py:521
